TPU v7x, 256 devices: a whole 4x4x8 slice. The times are simulated.
256 devices in a mesh: line: 8 (over z_lo, core), bus: 32 (over y, x, z_hi).
Axes of the slice: x: 4, y: 4, z: 8 (z_hi: 2, z_lo: 4; z = z_hi * 4 + z_lo), core: 2. Of those that a mesh axis runs over, the one named last changes fastest.
Arguments:
- injections: float32 [64, 69632], P(None, 'bus'), may hold values from -6 to 6
- transfer_factors: float32 [4096, 69632], P('line', 'bus'), may hold values from -0.0234375 to 0.0234375
- outage_factors: float32 [4096, 8192], P('line', 'bus'), may hold values from -1 to 1
- outage_line: int32 [8192], P('bus'), may hold values from 0 to 4095
- limit_table: int32 [4, 4096], P(None, 'line'), may hold values from 1 to 4
- scenario_tier: int32 [64], replicated, may hold values from 0 to 3
Outputs:
- injection_grad: float32 [64, 69632], P('line', 'bus')
- mean_penalty: float32 [64], replicated
All inputs are finite; a program needn't handle non-finite values.
Results may differ from a plain program's by a relative error of at most 0.0003.
Values sent between devices are 32-bit elements; how exact they have to be, the bound alone decides.
A program may use at most 64 MiB of HBM per device.

v0:
```python
import math

import jax
import jax.numpy as jnp
from jax import lax
from jax.sharding import PartitionSpec as P

LINES = 4096
OUTAGES = 8192


def body(injections, transfer_factors, outage_factors, outage_line, limit_table, scenario_tier):
    scenarios = injections.shape[0]
    line_rows = transfer_factors.shape[0]
    outage_cols = outage_factors.shape[1]
    partial_flows = jnp.dot(
        injections,
        transfer_factors.T,
        precision=lax.Precision.HIGHEST,
        preferred_element_type=jnp.float32,
    )
    line_flows = lax.psum(partial_flows, "bus")
    line_start = lax.axis_index("line") * line_rows
    local_index = outage_line - line_start
    selector = (local_index[None, :] == jnp.arange(line_rows, dtype=jnp.int32)[:, None]).astype(
        jnp.float32
    )
    every_flow = lax.all_gather(line_flows, "line", axis=1, tiled=True)
    outage_flows = jnp.take(every_flow, outage_line, axis=1)
    tier_onehot = (
        scenario_tier[:, None] == jnp.arange(limit_table.shape[0], dtype=jnp.int32)[None, :]
    ).astype(jnp.float32)
    limits = 0.4 * jnp.dot(
        tier_onehot,
        limit_table.astype(jnp.float32),
        precision=lax.Precision.HIGHEST,
        preferred_element_type=jnp.float32,
    )
    block_rows = math.gcd(scenarios, 16)
    num_blocks = scenarios // block_rows

    def one_block(values):
        flow_block, outage_block, limit_block = values
        post = flow_block[:, :, None] + outage_factors[None, :, :] * outage_block[:, None, :]
        excess = jnp.maximum(jnp.abs(post) - limit_block[:, :, None], 0.0)
        weight = 2.0 * excess * jnp.sign(post) / OUTAGES
        return (
            jnp.sum(excess * excess, axis=(1, 2)),
            jnp.sum(weight, axis=2),
            jnp.sum(weight * outage_factors[None, :, :], axis=1),
        )

    penalty, direct, back_part = lax.map(
        one_block,
        (
            line_flows.reshape(num_blocks, block_rows, line_rows),
            outage_flows.reshape(num_blocks, block_rows, outage_cols),
            limits.reshape(num_blocks, block_rows, line_rows),
        ),
    )
    penalty = penalty.reshape(scenarios)
    direct = direct.reshape(scenarios, line_rows)
    back_part = back_part.reshape(scenarios, outage_cols)
    back = lax.psum(back_part, "line")
    carried = jnp.dot(
        back, selector.T, precision=lax.Precision.HIGHEST, preferred_element_type=jnp.float32
    )
    flow_grad, penalty_sum = lax.psum((direct + carried, penalty), "bus")
    total_penalty = lax.psum(penalty, ("line", "bus"))
    mean_penalty = total_penalty / (LINES * OUTAGES)
    injection_grad = lax.psum_scatter(
        jnp.dot(
            flow_grad,
            transfer_factors,
            precision=lax.Precision.HIGHEST,
            preferred_element_type=jnp.float32,
        ),
        "line",
        scatter_dimension=0,
        tiled=True,
    )
    return (injection_grad, mean_penalty)


def solution(mesh):
    return jax.shard_map(
        body,
        mesh=mesh,
        in_specs=(
            P(None, "bus"),
            P("line", "bus"),
            P("line", "bus"),
            P("bus"),
            P(None, "line"),
            P(),
        ),
        out_specs=(P("line", "bus"), P()),
        check_vma=False,
    )
```

profile of v0, /device:TPU:1, one launch (start us, length us, event | category | flops | bytes accessed | tf_op | source)
XLA Modules:
  0.0 1058.1 jit_solution(12316503134355533745)
XLA Ops:
  7.3 1.0 copy-done
  8.2 7.2 fusion.3
  15.5 387.3 %all-reduce.6.cloned.1.call-done = f32[64,512]{1,0:T(8,128)} async-done(((f32[64,512]{1,0:T(8,128)}), f32[64,512]{1,0:T(8,128)}) %all-reduce.6.cloned.1.call-update) | async-done | bytes 131088 | tf_op jit(solution)/shard_map/psum | solution.py:22
  403.3 49.7 %all-gather.2.cloned.1.call-done = f32[64,4096]{1,0:T(8,128)} async-done(((f32[64,512]{1,0:T(8,128)}), f32[64,4096]{1,0:T(8,128)}) %all-gather.2.cloned.1.call-update) | async-done | bytes 1048592 | tf_op jit(solution)/shard_map/all_gather | solution.py:28
  453.0 1.8 copy.14
  454.8 0.7 gather_fusion
  455.7 40.5 %while.14 = (s32[]{:T(128)}, f32[4,16]{1,0:T(4,128)S(1)}, f32[4,16,512]{2,1,0:T(8,128)}, f32[4,16,256]{2,1,0:T(8,128)}, f32[4,16,512]{2,1,0:T(8,128)}, /*index=5...) while((s32[]{:T(128)}, f32[4,16]{1,0:T(4,128)S(1)}, ...), condition=%wide.region_5.6_spmd, body=%wide.region_1.5_spmd.sunk | while | flops 29478896 | bytes 2491697 | solution.py:53
  455.7 0.8 dynamic-slice_bitcast_fusion.5
  456.5 8.0 multiply_reduce_fusion.4
  464.5 0.6 bitcast_dynamic-update-slice_fusion.4
  465.8 0.8 dynamic-slice_bitcast_fusion.5
  466.6 8.0 multiply_reduce_fusion.4
  475.9 0.8 dynamic-slice_bitcast_fusion.5
  476.7 8.0 multiply_reduce_fusion.4
  484.8 0.6 bitcast_dynamic-update-slice_fusion.4
  486.0 0.8 dynamic-slice_bitcast_fusion.5
  486.8 8.0 multiply_reduce_fusion.4
  494.9 0.6 bitcast_dynamic-update-slice_fusion.4
  496.2 68.3 %all-reduce.8.cloned.1.call-done = f32[64,256]{1,0:T(8,128)} async-done(((f32[64,256]{1,0:T(8,128)}), f32[64,256]{1,0:T(8,128)}) %all-reduce.8.cloned.1.call-update) | async-done | bytes 65552 | tf_op jit(solution)/shard_map/psum | solution.py:64
  564.5 2.0 convolution_add_fusion
  566.6 385.1 %all-reduce.10.cloned.1.call-done = f32[64,512]{1,0:T(8,128)} async-done(((f32[64,512]{1,0:T(8,128)}), f32[64,512]{1,0:T(8,128)}) %all-reduce.10.cloned.1.call-update) | async-done | bytes 131088 | tf_op jit(solution)/shard_map/psum | solution.py:68
  951.7 5.9 fusion.4
  958.9 90.6 %psum.31 = f32[64]{0:T(128)S(1)} all-reduce(f32[64]{0:T(128)S(1)} %reshape.44), channel_id=1, replica_groups=mesh['line'=8,'bus'=32] {'line','bus'}, use_global_device_ids=true, to_apply=%region_9.10 | all-reduce | flops 64 | bytes 512 | tf_op jit(solution)/shard_map/psum | solution.py:69
  1050.0 1.5 constant_dynamic-slice_fusion
  (51 shorter events, 5.2 us)
Async XLA Ops:
  7.2 1.1 copy-start
  7.2 395.8 %copy-start.3 = (s32[256]{0:T(256)S(1)}, s32[256]{0:T(256)}, u32[]{:S(2)}) copy-start(s32[256]{0:T(256)} %param.11) | copy-start | bytes 3076
  7.2 395.8 %copy-start.2 = (s32[4,512]{1,0:T(4,128)S(1)}, s32[4,512]{1,0:T(4,128)}, u32[]{:S(2)}) copy-start(s32[4,512]{1,0:T(4,128)} %param.12) | copy-start | bytes 24580
  7.2 395.8 %copy-start.4 = (s32[64]{0:T(128)S(1)}, s32[64]{0:T(128)}, u32[]{:S(2)}) copy-start(s32[64]{0:T(128)} %param.13) | copy-start | bytes 772
  7.2 448.4 %copy-start.1 = (f32[512,256]{1,0:T(8,128)S(1)}, f32[512,256]{1,0:T(8,128)}, u32[]{:S(2)}) copy-start(f32[512,256]{1,0:T(8,128)} %param.10) | copy-start | bytes 1572868
  7.2 395.6 %all-reduce.6.cloned.1.call-start = ((), (), s32[]{:S(2)}) async-start(), calls=%async_computation | async-start | bytes 262144 | tf_op jit(solution)/shard_map/psum | solution.py:22
  15.5 437.5 %all-gather.2.cloned.1.call-start = ((), (), s32[]{:S(2)}) async-start(), calls=%async_computation.1 | async-start | bytes 1179648 | tf_op jit(solution)/shard_map/all_gather | solution.py:28
  402.9 161.7 %all-reduce.8.cloned.1.call-start = ((), (), s32[]{:S(2)}) async-start(), calls=%async_computation.2 | async-start | bytes 131072 | tf_op jit(solution)/shard_map/psum | solution.py:64
  496.1 461.5 %copy-start.5 = (u32[256]{0:T(256)S(1)}, u32[256]{0:T(256)}, u32[]{:S(2)}) copy-start(u32[256]{0:T(256)} %constant.60) | copy-start | bytes 3076
  496.2 455.5 %all-reduce.10.cloned.1.call-start = ((), (), s32[]{:S(2)}) async-start(), calls=%async_computation.3 | async-start | bytes 262144 | tf_op jit(solution)/shard_map/psum | solution.py:68
  566.5 483.5 %all-reduce.12.cloned.1.call-start = ((), (), s32[]{:S(2)}) async-start(), calls=%async_computation.4 | async-start | bytes 1114112
Sparse Core Ops, SparseCore 0:
  15.6 387.1 all-reduce.5
  404.8 48.1 all-gather.1
  496.3 68.2 all-reduce.7
  567.0 384.6 all-reduce.9
  957.7 82.7 all-reduce.11
where the time goes:
time: 1060 us
  waiting for transfers between devices  890 us (84%)
  blocking collectives  90.6 us (9%)
  other arithmetic  32.9 us (3%)
  matrix products  15.4 us (1%)
  between operations  14.6 us (1%)
  local copies, waits for them, and re-layouts  13.9 us (1%)
    psum x1, waiting for transfers between devices, body(): line_flows = lax.psum(partial_flows, 'bus')  387 us
    psum x1, waiting for transfers between devices, body(): flow_grad, penalty_sum = lax.psum((direct + carried, penalty), 'bus')  385 us
    psum x1, blocking collectives, body(): total_penalty = lax.psum(penalty, ('line', 'bus'))  90.6 us
    psum x1, waiting for transfers between devices, body(): back = lax.psum(back_part, 'line')  68.3 us
    all_gather x1, waiting for transfers between devices, body(): every_flow = lax.all_gather(line_flows, 'line', axis=1, tiled=True)  49.7 us
    reduce_sum x4, other arithmetic, one_block(): jnp.sum(weight * outage_factors[None, :, :], axis=1)  32.2 us
  transfers between devices with their start and end apart: 5, of which 4 were waited for; matrix products, arithmetic and copies ran while one was open for 0% of the time, Pallas kernels for 0%

commit v1 on v0

v1 whole, which is shorter than its diff:
```python
import jax
import jax.numpy as jnp
from jax import lax
from jax.experimental import pallas as pl
from jax.experimental.pallas import tpu as pltpu
from jax.sharding import PartitionSpec as P

LINES = 4096
OUTAGES = 8192
SCEN = 64
BUS_COLS = 2176
ROWS = 512
OUTS = 256
CHUNKS = ((0, 640), (640, 512), (1152, 512), (1664, 512))
F32 = jnp.float32
BF16 = jnp.bfloat16
NT = (((1,), (1,)), ((), ()))


def split(value):
    high = value.astype(BF16)
    return high, (value - high.astype(F32)).astype(BF16)


def kernel(
    tier_ref, inj_hbm, tf_hbm, w_hbm, ol_ref, table_ref, grad_ref, pen_ref,
    tf, tf_hi, tf_lo, inj, inj_hl, w, limit, sel,
    part, s1, s2_src, s2, ol_src, ol_all, s3_src, s3,
    flow_t, outage, direct_t, back, pen_acc,
    t1_src, t1, t2_src, t2, t3_src, t3, pen_src, pen1, pen2_src, pen2, back_hl,
    g_src, r1, r2_src, r2,
    load_sem, send_sem, recv_sem, core_send, core_recv, far_send, far_recv,
):
    i = lax.axis_index("line")
    j = lax.axis_index("bus")
    p = j // 2
    zh = lax.rem(j, 2)
    q = zh * 8 + i
    core = lax.rem(i, 2)
    z = i // 2
    half = lax.rem(p, 2)

    def plane_peer(d):
        other = lax.rem(p + d, 16)
        return other, (i, other * 2 + zh)

    def column_peer(d):
        other = lax.rem(q + d, 16)
        return other, (lax.rem(other, 8), p * 2 + other // 8)

    barrier = pltpu.get_barrier_semaphore()

    def greet(d, carry):
        for peer in (plane_peer, column_peer):
            pl.semaphore_signal(
                barrier, inc=1, device_id=peer(d)[1], device_id_type=pl.DeviceIdType.MESH
            )
        return carry

    loads = [pltpu.make_async_copy(inj_hbm, inj, load_sem.at[0])]
    for n in range(2):
        rows = pl.ds(n * 256, 256)
        loads.append(pltpu.make_async_copy(tf_hbm.at[rows], tf.at[rows], load_sem.at[1 + n]))
    loads.append(pltpu.make_async_copy(w_hbm, w, load_sem.at[3]))
    for copy in loads:
        copy.start()
    lax.fori_loop(1, 16, greet, 0)

    def send_all(peer, phase, source, target):
        def one(d, carry):
            other, device = peer(d)
            pltpu.make_async_remote_copy(
                src_ref=source(other),
                dst_ref=target,
                send_sem=send_sem.at[phase],
                recv_sem=recv_sem.at[phase],
                device_id=device,
                device_id_type=pl.DeviceIdType.MESH,
            ).start()
            return carry

        lax.fori_loop(1, 16, one, 0)

    def arrive(phase, buffer):
        view = buffer.at[pl.ds(0, 15)]
        pltpu.make_async_copy(view, view, recv_sem.at[phase]).wait()

    def sent(phase, buffer):
        view = buffer.at[pl.ds(0, 15)]
        pltpu.make_async_copy(view, view, send_sem.at[phase]).wait()

    for tier in range(4):
        for block in range(4):
            row = 0.4 * table_ref[tier : tier + 1, block * 128 : (block + 1) * 128].astype(F32)
            limit[tier, block * 128 : (block + 1) * 128, :] = jnp.broadcast_to(row, (128, 128)).T
    ol_src[...] = ol_ref[...].astype(F32)

    loads[0].wait()
    inj_hi, inj_lo = split(inj[...])
    inj_hl[0:SCEN, :] = inj_hi
    inj_hl[SCEN : 2 * SCEN, :] = inj_lo
    for n in range(2):
        loads[1 + n].wait()

        def cut(step, carry):
            rows = pl.ds(pl.multiple_of(n * 256 + step * 32, 32), 32)
            high, low = split(tf[rows, :])
            tf_hi[rows, :] = high
            tf_lo[rows, :] = low
            return carry

        lax.fori_loop(0, 8, cut, 0)
        rows = slice(n * 256, (n + 1) * 256)
        both = lax.dot_general(inj_hl[...], tf_hi[rows, :], NT, preferred_element_type=F32)
        low = lax.dot_general(inj_hl[0:SCEN, :], tf_lo[rows, :], NT, preferred_element_type=F32)
        flows = both[0:SCEN] + (both[SCEN : 2 * SCEN] + low)
        for group in range(8):
            part[2 * group + n] = flows[group * 8 : (group + 1) * 8]

    pl.semaphore_wait(barrier, 30)
    send_all(plane_peer, 0, lambda other: part.at[other], s1.at[p])
    send_all(plane_peer, 1, lambda other: ol_src, ol_all.at[p])
    s1[p] = part[p]
    ol_all[p] = ol_src[...]
    loads[3].wait()
    direct_t[...] = jnp.zeros_like(direct_t)
    arrive(0, s1)
    s2_src[...] = jnp.sum(s1[...], axis=0)
    send_all(column_peer, 2, lambda other: s2_src, s2.at[q])
    s2[q] = s2_src[...]
    arrive(1, ol_all)

    def pick(block, carry):
        base = (block * 512 + half * 256).astype(F32)
        names = lax.broadcasted_iota(jnp.int32, (256, 256), 0).astype(F32) + base
        for group in range(16):
            hit = names == jnp.broadcast_to(ol_all[group], (256, 256))
            sel[block, :, group * 256 : (group + 1) * 256] = jnp.where(hit, 1.0, 0.0).astype(BF16)
        return carry

    lax.fori_loop(0, 4, pick, 0)
    arrive(2, s2)
    full = [s2[b] + s2[8 + b] for b in range(8)]
    sources = [(b * 4 + k, full[b][:, k * 128 : (k + 1) * 128]) for b in range(8) for k in range(2)]

    def choose(group, carry):
        for k in range(2):
            where = jnp.broadcast_to(ol_all[group, :, k * 128 : (k + 1) * 128], (8, 128)).astype(jnp.int32)
            lane = jnp.bitwise_and(where, 127)
            tile = jnp.right_shift(where, 7) - 2 * half
            out = jnp.zeros((8, 128), F32)
            for name, source in sources:
                out = jnp.where(tile == name, jnp.take_along_axis(source, lane, axis=1), out)
            s3_src[group, 1, :, k * 128 : (k + 1) * 128] = out
        s3_src[group, 0] = s2[i] + s2[8 + i]
        return carry

    lax.fori_loop(0, 16, choose, 0)
    send_all(plane_peer, 3, lambda other: s3_src.at[other], s3.at[p])
    s3[p] = s3_src[p]
    lax.fori_loop(4, 8, pick, 0)
    arrive(3, s3)
    for h in range(2):
        tiles = jnp.concatenate([s3[2 * g + h, 0] for g in range(8)], axis=0)
        flow_t[h * 256 : (h + 1) * 256, 0:SCEN] = tiles.T
    for g in range(8):
        outage[g * 8 : (g + 1) * 8, :] = s3[2 * g, 1] + s3[2 * g + 1, 1]

    lanes = lax.broadcasted_iota(jnp.int32, (8, 128), 1)
    zero = jnp.zeros((8, 128), F32)

    def scenarios(group, carry):
        block = pl.ds(pl.multiple_of(group * 8, 8), 8)
        tile = outage[block, :]
        done = []
        for part_of in range(2):
            first = [part_of * 4 + u for u in range(4)]
            near = [
                [jnp.broadcast_to(tile[u : u + 1, k * 128 : (k + 1) * 128], (8, 128)) for k in range(2)]
                for u in first
            ]
            index = [jnp.full((8, 128), group * 8 + u, jnp.int32) for u in first]
            tiers = [tier_ref[group * 8 + u] for u in first]

            def lines(step, sums):
                sums = list(sums)
                for v in range(4):
                    rows = pl.ds(pl.multiple_of(step * 32 + v * 8, 8), 8)
                    factors = (w[rows, 0:128], w[rows, 128:256])
                    flow = flow_t[rows, :]
                    kept = direct_t[rows, :]
                    for u in range(4):
                        top = limit[tiers[u], rows, :]
                        base = jnp.take_along_axis(flow, index[u], axis=1)
                        over = []
                        for k in range(2):
                            post = base + factors[k] * near[u][k]
                            over.append(post - jnp.minimum(jnp.maximum(post, -top), top))
                            sums[3 * u + k] = sums[3 * u + k] + over[k] * factors[k]
                        sums[3 * u + 2] = sums[3 * u + 2] + (over[0] * over[0] + over[1] * over[1])
                        total = jnp.sum(over[0] + over[1], axis=1, keepdims=True)
                        kept = jnp.where(lanes == index[u], total, kept)
                    direct_t[rows, :] = kept
                return tuple(sums)

            done.extend(lax.fori_loop(0, 16, lines, (zero,) * 12))

        def rows_of(k):
            return jnp.concatenate(
                [jnp.sum(done[3 * u + k], axis=0, keepdims=True) for u in range(8)], axis=0
            )

        back[block, 0:128] = rows_of(0)
        back[block, 128:256] = rows_of(1)
        pen_acc[block, :] = rows_of(2)
        return carry

    lax.fori_loop(0, 8, scenarios, 0)

    for h in range(2):
        turned = direct_t[h * 256 : (h + 1) * 256, :].T
        for g in range(8):
            t1_src[2 * g + h, 0] = turned[g * 8 : (g + 1) * 8, :]
            t1_src[2 * g + h, 1] = back[g * 8 : (g + 1) * 8, :]
    send_all(plane_peer, 4, lambda other: t1_src.at[other], t1.at[p])
    t1[p] = t1_src[p]
    pen_src[:, 0:SCEN] = jnp.sum(pen_acc[...].T, axis=0, keepdims=True)
    pen_src[:, SCEN:128] = jnp.zeros((1, 64), F32)
    send_all(plane_peer, 5, lambda other: pen_src, pen1.at[p])
    pen1[p] = pen_src[...]
    arrive(4, t1)
    for g in range(16):
        high, low = split(t1[g, 1])
        back_hl[:, g * 256 : (g + 1) * 256] = jnp.concatenate([high, low], axis=0)

    def spread(block, carry):
        both = lax.dot_general(back_hl[...], sel[block], NT, preferred_element_type=F32)
        t2_src[block] = both[0:8] + both[8:16]
        return carry

    lax.fori_loop(0, 8, spread, 0)
    t2_src[i] = t2_src[i] + jnp.sum(t1[:, 0], axis=0)
    send_all(column_peer, 6, lambda other: t2_src.at[lax.rem(other, 8)], t2.at[q])
    t2[q] = t2_src[i]
    arrive(5, pen1)
    pen2_src[...] = jnp.sum(pen1[...], axis=0)
    send_all(column_peer, 7, lambda other: pen2_src, pen2.at[q])
    pen2[q] = pen2_src[...]
    arrive(6, t2)
    t3_src[...] = jnp.sum(t2[...], axis=0) * (2.0 / OUTAGES)
    send_all(plane_peer, 8, lambda other: t3_src, t3.at[p])
    t3[p] = t3_src[...]
    arrive(7, pen2)
    pen_ref[...] = jnp.sum(pen2[...], axis=0) * (1.0 / (LINES * OUTAGES))
    arrive(8, t3)

    grad = jnp.concatenate(
        [jnp.concatenate([t3[2 * g + h] for g in range(8)], axis=0) for h in range(2)], axis=1
    )
    grad_hi, grad_lo = split(grad)
    grad_hl = jnp.concatenate([grad_hi, grad_lo], axis=0)
    twin = (i + 1 - 2 * core, j)

    def core_copy(n):
        start, width = CHUNKS[n]
        cols = pl.ds(start, width)
        return pltpu.make_async_remote_copy(
            src_ref=g_src.at[1 - core, :, :, cols],
            dst_ref=r1.at[:, :, cols],
            send_sem=core_send.at[n],
            recv_sem=core_recv.at[n],
            device_id=twin,
            device_id_type=pl.DeviceIdType.MESH,
        )

    def far_copy(n, d):
        start, width = CHUNKS[n]
        cols = pl.ds(start, width)
        other = lax.rem(z + d, 4)
        return pltpu.make_async_remote_copy(
            src_ref=r2_src.at[other, :, cols],
            dst_ref=r2.at[z, :, cols],
            send_sem=far_send.at[n, d - 1],
            recv_sem=far_recv.at[n, d - 1],
            device_id=(other * 2 + core, j),
            device_id_type=pl.DeviceIdType.MESH,
        )

    def pass_on(n):
        start, width = CHUNKS[n]
        cols = slice(start, start + width)
        core_copy(n).wait()
        r2_src[:, :, cols] = g_src[core, :, :, cols] + r1[:, :, cols]
        for d in range(1, 4):
            far_copy(n, d).start()

    for n, (start, width) in enumerate(CHUNKS):
        cols = slice(start, start + width)
        both = jnp.dot(grad_hl, tf_hi[:, cols], preferred_element_type=F32)
        low = jnp.dot(grad_hi, tf_lo[:, cols], preferred_element_type=F32)
        out = both[0:SCEN] + (both[SCEN : 2 * SCEN] + low)
        for a in range(4):
            for c in range(2):
                row = (2 * a + c) * 8
                g_src[c, a, :, cols] = out[row : row + 8]
        core_copy(n).start()
        if n > 0:
            pass_on(n - 1)
    pass_on(len(CHUNKS) - 1)
    r2[z] = r2_src[z]
    for n in range(len(CHUNKS)):
        for d in range(1, 4):
            far_copy(n, d).wait()
    grad_ref[...] = (r2[0] + r2[1]) + (r2[2] + r2[3])
    for phase, buffer in enumerate((s1, ol_all, s2, s3, t1, pen1, t2, pen2, t3)):
        sent(phase, buffer)


def body(injections, transfer_factors, outage_factors, outage_line, limit_table, scenario_tier):
    tile = (8, 256)
    vmem = pltpu.VMEM
    scratch = [
        vmem((ROWS, BUS_COLS), F32),
        vmem((ROWS, BUS_COLS), BF16),
        vmem((ROWS, BUS_COLS), BF16),
        vmem((SCEN, BUS_COLS), F32),
        vmem((2 * SCEN, BUS_COLS), BF16),
        vmem((ROWS, OUTS), F32),
        vmem((4, ROWS, 128), F32),
        vmem((8, 256, 4096), BF16),
        vmem((16,) + tile, F32),
        vmem((16,) + tile, F32),
        vmem(tile, F32),
        vmem((16,) + tile, F32),
        vmem((1, OUTS), F32),
        vmem((16, 1, OUTS), F32),
        vmem((16, 2) + tile, F32),
        vmem((16, 2) + tile, F32),
        vmem((ROWS, 128), F32),
        vmem((SCEN, OUTS), F32),
        vmem((ROWS, 128), F32),
        vmem((SCEN, OUTS), F32),
        vmem((SCEN, 128), F32),
        vmem((16, 2) + tile, F32),
        vmem((16, 2) + tile, F32),
        vmem((8,) + tile, F32),
        vmem((16,) + tile, F32),
        vmem(tile, F32),
        vmem((16,) + tile, F32),
        vmem((1, 128), F32),
        vmem((16, 1, 128), F32),
        vmem((1, 128), F32),
        vmem((16, 1, 128), F32),
        vmem((16, 4096), BF16),
        vmem((2, 4, 8, BUS_COLS), F32),
        vmem((4, 8, BUS_COLS), F32),
        vmem((4, 8, BUS_COLS), F32),
        vmem((4, 8, BUS_COLS), F32),
        pltpu.SemaphoreType.DMA((4,)),
        pltpu.SemaphoreType.DMA((9,)),
        pltpu.SemaphoreType.DMA((9,)),
        pltpu.SemaphoreType.DMA((4,)),
        pltpu.SemaphoreType.DMA((4,)),
        pltpu.SemaphoreType.DMA((4, 3)),
        pltpu.SemaphoreType.DMA((4, 3)),
    ]
    hbm = pl.BlockSpec(memory_space=pl.ANY)
    whole = pl.BlockSpec(memory_space=pltpu.VMEM)
    grad, penalty = pl.pallas_call(
        kernel,
        out_shape=(
            jax.ShapeDtypeStruct((8, BUS_COLS), F32),
            jax.ShapeDtypeStruct((1, 128), F32),
        ),
        in_specs=[pl.BlockSpec(memory_space=pltpu.SMEM), hbm, hbm, hbm, whole, whole],
        out_specs=(whole, whole),
        scratch_shapes=scratch,
        compiler_params=pltpu.CompilerParams(
            collective_id=0, has_side_effects=True, vmem_limit_bytes=60 << 20
        ),
        name="overload",
    )(
        scenario_tier,
        injections,
        transfer_factors,
        outage_factors,
        outage_line.reshape(1, OUTS),
        limit_table,
    )
    return grad, penalty[0, :SCEN]


def solution(mesh):
    return jax.shard_map(
        body,
        mesh=mesh,
        in_specs=(
            P(None, "bus"),
            P("line", "bus"),
            P("line", "bus"),
            P("bus"),
            P(None, "line"),
            P(),
        ),
        out_specs=(P("line", "bus"), P()),
        check_vma=False,
    )
```

time: 1060 us -> 215 us (0.20)
  waiting for transfers between devices: 890 us -> 0 us
  Pallas kernels: 0 us -> 212 us
  blocking collectives: 90.6 us -> 0 us
  other arithmetic: 32.9 us -> 0 us
  matrix products: 15.4 us -> 0 us
  between operations: 14.6 us -> 0.64 us
  local copies, waits for them, and re-layouts: 13.9 us -> 2.63 us
    psum x3 -> x0, waiting for transfers between devices: 841 us -> none  [the longest x1 387 us: body(): line_flows = lax.psum(partial_flows, 'bus')]
    pallas_call x0 -> x1, Pallas kernels: none -> 212 us  [body(): pl.pallas_call(kernel, out_shape=(jax.ShapeDtypeStruct((8, BUS_COLS), F32...]
    psum x1 -> x0, blocking collectives: 90.6 us -> none  [body(): total_penalty = lax.psum(penalty, ('line', 'bus'))]
    all_gather x1 -> x0, waiting for transfers between devices: 49.7 us -> none  [body(): every_flow = lax.all_gather(line_flows, 'line', axis=1, tiled=True)]
    reduce_sum x4 -> x0, other arithmetic: 32.2 us -> none  [one_block(): jnp.sum(weight * outage_factors[None, :, :], axis=1)]
    dot_general x4 -> x0, matrix products: 15.4 us -> none  [the longest x1 7.25 us: body(): jnp.dot(injections, transfer_factors.T, precision=lax.Precision.HIGHEST,...]
  transfers between devices with their start and end apart: 5 -> 0, of which waited for: 4 -> 0; matrix products, arithmetic and copies ran while one was open for 0% -> 0% of each run, Pallas kernels for 0% -> 0%
where the time goes in v1:
time: 215 us
  Pallas kernels  212 us (99%)
  local copies, waits for them, and re-layouts  2.63 us (1%)
    pallas_call x1, Pallas kernels, body(): pl.pallas_call(kernel, out_shape=(jax.ShapeDtypeStruct((8, BUS_COLS), F32...  212 us

profile of v1, /device:TPU:1, one launch (start us, length us, event | category | flops | bytes accessed | tf_op | source)
XLA Modules:
  0.0 215.1 jit_solution(1278100583337683387)
XLA Ops:
  0.6 211.9 %overload.1 = (f32[8,2176]{1,0:T(8,128)}, f32[1,128]{1,0:T(1,128)}) custom-call(s32[64]{0:T(128)} %tier_ref.1, f32[64,2176]{1,0:T(8,128)} %inj_hbm.1, f32[512,2176]{1,0:T(8,128)} %tf_hbm.1, f32[512,256]{1,0:T(8,128)} %w_hbm.1, s32[1,256]{1,0:T(1,128)} %bitcast.3, s32[4,512]{1,0:T(4,128)} %table_ref.1), custom_call_target="tpu_custom_call" | custom-call | tf_op jit(solution)/shard_map/overload/pallas_call | solution.py:369
  212.5 1.1 slice_bitcast_fusion
  213.6 1.5 copy.9

commit v2 on v1

--- a/solution.py
+++ b/solution.py
@@ -24,10 +24,10 @@
 
 def kernel(
     tier_ref, inj_hbm, tf_hbm, w_hbm, ol_ref, table_ref, grad_ref, pen_ref,
-    tf, tf_hi, tf_lo, inj, inj_hl, w, limit, sel,
+    tf, tf_hi, tf_lo, inj, inj_hl, w, w_t, w_parts, w_wide, limit_t, lane_hit, spread_in,
     part, s1, s2_src, s2, ol_src, ol_all, s3_src, s3,
-    flow_t, outage, direct_t, back, pen_acc,
-    t1_src, t1, t2_src, t2, t3_src, t3, pen_src, pen1, pen2_src, pen2, back_hl,
+    flow_t, outage_t, direct_t, back_rows, back_t,
+    t1_src, t1, t2_src, t2, t3_src, t3, pen_src, pen1, pen2_src, pen2,
     g_src, r1, r2_src, r2,
     load_sem, send_sem, recv_sem, core_send, core_recv, far_send, far_recv,
 ):
@@ -89,10 +89,21 @@
         view = buffer.at[pl.ds(0, 15)]
         pltpu.make_async_copy(view, view, send_sem.at[phase]).wait()
 
-    for tier in range(4):
-        for block in range(4):
-            row = 0.4 * table_ref[tier : tier + 1, block * 128 : (block + 1) * 128].astype(F32)
-            limit[tier, block * 128 : (block + 1) * 128, :] = jnp.broadcast_to(row, (128, 128)).T
+    tiers = jnp.concatenate([tier_ref[...], tier_ref[...]], axis=1)
+    left = lax.broadcasted_iota(jnp.int32, (128, 128), 1) < SCEN
+    for block in range(2):
+        rows = slice(block * 128, (block + 1) * 128)
+        value = jnp.zeros((128, 128), F32)
+        for tier in range(4):
+            pair = [
+                jnp.broadcast_to(
+                    0.4 * table_ref[tier : tier + 1, h * 256 + block * 128 : h * 256 + block * 128 + 128].astype(F32),
+                    (128, 128),
+                ).T
+                for h in range(2)
+            ]
+            value = jnp.where(tiers == tier, jnp.where(left, pair[0], pair[1]), value)
+        limit_t[rows, :] = value
     ol_src[...] = ol_ref[...].astype(F32)
 
     loads[0].wait()
@@ -117,28 +128,53 @@
         for group in range(8):
             part[2 * group + n] = flows[group * 8 : (group + 1) * 8]
 
+    key_row = lax.broadcasted_iota(jnp.int32, (256, 256), 0)
+    key_col = lax.broadcasted_iota(jnp.int32, (256, 256), 1)
+    same_half = jnp.bitwise_and(jnp.right_shift(key_row, 5) - jnp.right_shift(key_col, 6), 1) == 0
+    key = jnp.where(same_half, jnp.bitwise_and(key_row, 31) - jnp.right_shift(key_col, 7), -1)
+
+    def widen_start():
+        w_t[...] = w[...].T
+
+        def group(g, carry):
+            piece = w_t[pl.ds(pl.multiple_of(g * 32, 32), 32), :]
+            high = piece.astype(BF16).astype(F32)
+            rest = piece - high
+            middle = rest.astype(BF16).astype(F32)
+            stack = [
+                value[:, h * 256 : (h + 1) * 256]
+                for value in (high, middle, rest - middle)
+                for h in range(2)
+            ]
+            stack.append(jnp.zeros((64, 256), F32))
+            w_parts[g] = jnp.concatenate(stack, axis=0).T.astype(BF16)
+            return carry
+
+        lax.fori_loop(0, 8, group, 0)
+
+    def widen(step, carry):
+        ones = jnp.where(key == 2 * step, 1.0, 0.0).astype(BF16)
+        for g in range(8):
+            wide = jnp.dot(w_parts[g], ones, preferred_element_type=F32)
+            w_wide[g * 32 + 2 * step] = wide[:, 0:128]
+            w_wide[g * 32 + 2 * step + 1] = wide[:, 128:256]
+        return carry
+
     pl.semaphore_wait(barrier, 30)
     send_all(plane_peer, 0, lambda other: part.at[other], s1.at[p])
     send_all(plane_peer, 1, lambda other: ol_src, ol_all.at[p])
     s1[p] = part[p]
     ol_all[p] = ol_src[...]
     loads[3].wait()
-    direct_t[...] = jnp.zeros_like(direct_t)
+    widen_start()
+    lax.fori_loop(0, 4, widen, 0)
     arrive(0, s1)
     s2_src[...] = jnp.sum(s1[...], axis=0)
     send_all(column_peer, 2, lambda other: s2_src, s2.at[q])
     s2[q] = s2_src[...]
     arrive(1, ol_all)
 
-    def pick(block, carry):
-        base = (block * 512 + half * 256).astype(F32)
-        names = lax.broadcasted_iota(jnp.int32, (256, 256), 0).astype(F32) + base
-        for group in range(16):
-            hit = names == jnp.broadcast_to(ol_all[group], (256, 256))
-            sel[block, :, group * 256 : (group + 1) * 256] = jnp.where(hit, 1.0, 0.0).astype(BF16)
-        return carry
-
-    lax.fori_loop(0, 4, pick, 0)
+    lax.fori_loop(4, 10, widen, 0)
     arrive(2, s2)
     full = [s2[b] + s2[8 + b] for b in range(8)]
     sources = [(b * 4 + k, full[b][:, k * 128 : (k + 1) * 128]) for b in range(8) for k in range(2)]
@@ -158,87 +194,93 @@
     lax.fori_loop(0, 16, choose, 0)
     send_all(plane_peer, 3, lambda other: s3_src.at[other], s3.at[p])
     s3[p] = s3_src[p]
-    lax.fori_loop(4, 8, pick, 0)
+    lax.fori_loop(10, 16, widen, 0)
     arrive(3, s3)
+    tiles = jnp.concatenate([s3[2 * g + h, 0] for h in range(2) for g in range(8)], axis=0)
+    flow_t[...] = tiles.T
+    picked = jnp.concatenate([s3[2 * g, 1] + s3[2 * g + 1, 1] for g in range(8)], axis=0)
+    outage_t[...] = jnp.concatenate([picked, picked], axis=0).T
+
+    penalty = jnp.zeros((8, 128), F32)
+    for block in range(4):
+        slabs = [slice(block * 64 + v * 8, block * 64 + v * 8 + 8) for v in range(8)]
+        flow = [flow_t[rows, :] for rows in slabs]
+        top = [limit_t[rows, :] for rows in slabs]
+        low = [-value for value in top]
+
+        def outages(step, carry):
+            direct = list(carry[:8])
+            squares = carry[8]
+            eight = pl.ds(pl.multiple_of(step * 8, 8), 8)
+            near = outage_t[eight, :]
+            sums = []
+            for u in range(8):
+                name = step * 8 + u
+                here = jnp.broadcast_to(near[u : u + 1, :], (8, 128))
+                back = None
+                for v in range(8):
+                    factor = w_wide[name, slabs[v], :]
+                    post = factor * here + flow[v]
+                    over = post - jnp.minimum(jnp.maximum(post, low[v]), top[v])
+                    direct[v] = direct[v] + over
+                    term = over * factor
+                    back = term if back is None else back + term
+                    squares = squares + over * over
+                if block > 0:
+                    back = back + back_rows[name]
+                if block < 3:
+                    back_rows[name] = back
+                else:
+                    sums.append(jnp.sum(back, axis=0, keepdims=True))
+            if block == 3:
+                back_t[eight, :] = jnp.concatenate(sums, axis=0)
+            return tuple(direct) + (squares,)
+
+        start = tuple(jnp.zeros((8, 128), F32) for _ in range(8)) + (penalty,)
+        result = lax.fori_loop(0, 32, outages, start)
+        for v in range(8):
+            direct_t[slabs[v], :] = result[v]
+        penalty = result[8]
+
+    direct = direct_t[...].T
+    back = back_t[...].T
+    back = back[0:SCEN] + back[SCEN : 2 * SCEN]
     for h in range(2):
-        tiles = jnp.concatenate([s3[2 * g + h, 0] for g in range(8)], axis=0)
-        flow_t[h * 256 : (h + 1) * 256, 0:SCEN] = tiles.T
-    for g in range(8):
-        outage[g * 8 : (g + 1) * 8, :] = s3[2 * g, 1] + s3[2 * g + 1, 1]
-
-    lanes = lax.broadcasted_iota(jnp.int32, (8, 128), 1)
-    zero = jnp.zeros((8, 128), F32)
-
-    def scenarios(group, carry):
-        block = pl.ds(pl.multiple_of(group * 8, 8), 8)
-        tile = outage[block, :]
-        done = []
-        for part_of in range(2):
-            first = [part_of * 4 + u for u in range(4)]
-            near = [
-                [jnp.broadcast_to(tile[u : u + 1, k * 128 : (k + 1) * 128], (8, 128)) for k in range(2)]
-                for u in first
-            ]
-            index = [jnp.full((8, 128), group * 8 + u, jnp.int32) for u in first]
-            tiers = [tier_ref[group * 8 + u] for u in first]
-
-            def lines(step, sums):
-                sums = list(sums)
-                for v in range(4):
-                    rows = pl.ds(pl.multiple_of(step * 32 + v * 8, 8), 8)
-                    factors = (w[rows, 0:128], w[rows, 128:256])
-                    flow = flow_t[rows, :]
-                    kept = direct_t[rows, :]
-                    for u in range(4):
-                        top = limit[tiers[u], rows, :]
-                        base = jnp.take_along_axis(flow, index[u], axis=1)
-                        over = []
-                        for k in range(2):
-                            post = base + factors[k] * near[u][k]
-                            over.append(post - jnp.minimum(jnp.maximum(post, -top), top))
-                            sums[3 * u + k] = sums[3 * u + k] + over[k] * factors[k]
-                        sums[3 * u + 2] = sums[3 * u + 2] + (over[0] * over[0] + over[1] * over[1])
-                        total = jnp.sum(over[0] + over[1], axis=1, keepdims=True)
-                        kept = jnp.where(lanes == index[u], total, kept)
-                    direct_t[rows, :] = kept
-                return tuple(sums)
-
-            done.extend(lax.fori_loop(0, 16, lines, (zero,) * 12))
-
-        def rows_of(k):
-            return jnp.concatenate(
-                [jnp.sum(done[3 * u + k], axis=0, keepdims=True) for u in range(8)], axis=0
-            )
-
-        back[block, 0:128] = rows_of(0)
-        back[block, 128:256] = rows_of(1)
-        pen_acc[block, :] = rows_of(2)
-        return carry
-
-    lax.fori_loop(0, 8, scenarios, 0)
-
-    for h in range(2):
-        turned = direct_t[h * 256 : (h + 1) * 256, :].T
         for g in range(8):
-            t1_src[2 * g + h, 0] = turned[g * 8 : (g + 1) * 8, :]
+            t1_src[2 * g + h, 0] = direct[h * SCEN + g * 8 : h * SCEN + g * 8 + 8, :]
             t1_src[2 * g + h, 1] = back[g * 8 : (g + 1) * 8, :]
     send_all(plane_peer, 4, lambda other: t1_src.at[other], t1.at[p])
     t1[p] = t1_src[p]
-    pen_src[:, 0:SCEN] = jnp.sum(pen_acc[...].T, axis=0, keepdims=True)
-    pen_src[:, SCEN:128] = jnp.zeros((1, 64), F32)
+    pen_src[...] = jnp.sum(penalty, axis=0, keepdims=True)
     send_all(plane_peer, 5, lambda other: pen_src, pen1.at[p])
     pen1[p] = pen_src[...]
+    def mark(group, carry):
+        lane = jnp.bitwise_and(jnp.broadcast_to(ol_all[group], (128, 256)).astype(jnp.int32), 127)
+        hit = lane == lax.broadcasted_iota(jnp.int32, (128, 256), 0)
+        lane_hit[group] = jnp.where(hit, 1.0, 0.0).astype(BF16)
+        return carry
+
+    lax.fori_loop(0, 16, mark, 0)
     arrive(4, t1)
-    for g in range(16):
-        high, low = split(t1[g, 1])
-        back_hl[:, g * 256 : (g + 1) * 256] = jnp.concatenate([high, low], axis=0)
-
-    def spread(block, carry):
-        both = lax.dot_general(back_hl[...], sel[block], NT, preferred_element_type=F32)
-        t2_src[block] = both[0:8] + both[8:16]
+
+    def sort(group, carry):
+        high, low = split(t1[group, 1])
+        both = jnp.concatenate([high.astype(F32), low.astype(F32)], axis=0)
+        tile = jnp.right_shift(jnp.broadcast_to(ol_all[group], (16, 256)).astype(jnp.int32), 7) - 2 * half
+        for t in range(16):
+            name = (t // 2) * 4 + t % 2
+            spread_in[group, t * 16 : (t + 1) * 16, :] = jnp.where(tile == name, both, 0.0).astype(BF16)
         return carry
 
-    lax.fori_loop(0, 8, spread, 0)
+    lax.fori_loop(0, 16, sort, 0)
+    total = jnp.zeros((256, 128), F32)
+    for group in range(16):
+        total = total + lax.dot_general(
+            spread_in[group], lane_hit[group], NT, preferred_element_type=F32
+        )
+    for t in range(16):
+        cols = slice((t % 2) * 128, (t % 2) * 128 + 128)
+        t2_src[t // 2, :, cols] = total[t * 16 : t * 16 + 8] + total[t * 16 + 8 : t * 16 + 16]
     t2_src[i] = t2_src[i] + jnp.sum(t1[:, 0], axis=0)
     send_all(column_peer, 6, lambda other: t2_src.at[lax.rem(other, 8)], t2.at[q])
     t2[q] = t2_src[i]
@@ -251,7 +293,8 @@
     send_all(plane_peer, 8, lambda other: t3_src, t3.at[p])
     t3[p] = t3_src[...]
     arrive(7, pen2)
-    pen_ref[...] = jnp.sum(pen2[...], axis=0) * (1.0 / (LINES * OUTAGES))
+    both = jnp.sum(pen2[...], axis=0) * (1.0 / (LINES * OUTAGES))
+    pen_ref[...] = both[:, 0:SCEN] + both[:, SCEN:128]
     arrive(8, t3)
 
     grad = jnp.concatenate(
@@ -326,8 +369,12 @@
         vmem((SCEN, BUS_COLS), F32),
         vmem((2 * SCEN, BUS_COLS), BF16),
         vmem((ROWS, OUTS), F32),
-        vmem((4, ROWS, 128), F32),
-        vmem((8, 256, 4096), BF16),
+        vmem((OUTS, ROWS), F32),
+        vmem((8, 256, 256), BF16),
+        vmem((OUTS, 256, 128), F32),
+        vmem((256, 128), F32),
+        vmem((16, 128, 256), BF16),
+        vmem((16, 256, 256), BF16),
         vmem((16,) + tile, F32),
         vmem((16,) + tile, F32),
         vmem(tile, F32),
@@ -336,11 +383,11 @@
         vmem((16, 1, OUTS), F32),
         vmem((16, 2) + tile, F32),
         vmem((16, 2) + tile, F32),
-        vmem((ROWS, 128), F32),
-        vmem((SCEN, OUTS), F32),
-        vmem((ROWS, 128), F32),
-        vmem((SCEN, OUTS), F32),
-        vmem((SCEN, 128), F32),
+        vmem((256, 128), F32),
+        vmem((OUTS, 128), F32),
+        vmem((256, 128), F32),
+        vmem((OUTS, 8, 128), F32),
+        vmem((OUTS, 128), F32),
         vmem((16, 2) + tile, F32),
         vmem((16, 2) + tile, F32),
         vmem((8,) + tile, F32),
@@ -351,7 +398,6 @@
         vmem((16, 1, 128), F32),
         vmem((1, 128), F32),
         vmem((16, 1, 128), F32),
-        vmem((16, 4096), BF16),
         vmem((2, 4, 8, BUS_COLS), F32),
         vmem((4, 8, BUS_COLS), F32),
         vmem((4, 8, BUS_COLS), F32),
@@ -370,9 +416,9 @@
         kernel,
         out_shape=(
             jax.ShapeDtypeStruct((8, BUS_COLS), F32),
-            jax.ShapeDtypeStruct((1, 128), F32),
+            jax.ShapeDtypeStruct((1, SCEN), F32),
         ),
-        in_specs=[pl.BlockSpec(memory_space=pltpu.SMEM), hbm, hbm, hbm, whole, whole],
+        in_specs=[whole, hbm, hbm, hbm, whole, whole],
         out_specs=(whole, whole),
         scratch_shapes=scratch,
         compiler_params=pltpu.CompilerParams(
@@ -380,14 +426,14 @@
         ),
         name="overload",
     )(
-        scenario_tier,
+        scenario_tier.reshape(1, SCEN),
         injections,
         transfer_factors,
         outage_factors,
         outage_line.reshape(1, OUTS),
         limit_table,
     )
-    return grad, penalty[0, :SCEN]
+    return grad, penalty.reshape(SCEN)
 
 
 def solution(mesh):

time: 215 us -> 74.8 us (0.35)
  Pallas kernels: 212 us -> 71.3 us
    pallas_call x1, Pallas kernels: 212 us -> 71.3 us  [body(): pl.pallas_call(kernel, out_shape=(jax.ShapeDtypeStruct((8, BUS_COLS), F32...]
where the time goes in v2:
time: 74.8 us; the launch traced here: 74.6 us
  Pallas kernels  71.3 us (95%)
  local copies, waits for them, and re-layouts  2.63 us (4%)
    pallas_call x1, Pallas kernels, body(): pl.pallas_call(kernel, out_shape=(jax.ShapeDtypeStruct((8, BUS_COLS), F32...  71.3 us
    unnamed x2, local copies, waits for them, and re-layouts  2.63 us

profile of v2, /device:TPU:1, one launch (start us, length us, event | category | flops | bytes accessed | tf_op | source)
XLA Modules:
  0.0 74.6 jit_solution(6511954276376708944)
XLA Ops:
  0.6 71.3 %overload.1 = (f32[8,2176]{1,0:T(8,128)}, f32[1,64]{1,0:T(1,128)}) custom-call(s32[1,64]{1,0:T(1,128)} %bitcast.4, f32[64,2176]{1,0:T(8,128)} %inj_hbm.1, f32[512,2176]{1,0:T(8,128)} %tf_hbm.1, f32[512,256]{1,0:T(8,128)} %w_hbm.1, s32[1,256]{1,0:T(1,128)} %bitcast.3, s32[4,512]{1,0:T(4,128)} %table_ref.1), custom_call_target="tpu_custom_call" | custom-call | tf_op jit(solution)/shard_map/overload/pallas_call | solution.py:415
  72.0 1.5 %copy.10 = f32[8,2176]{1,0:T(8,128)} copy(f32[8,2176]{1,0:T(8,128)} %get-tuple-element.8) | data formatting | bytes 139264
  73.5 1.1 %copy.11 = f32[64]{0:T(128)} copy(f32[64]{0:T(128)} %bitcast.5) | data formatting | bytes 512

commit v3 on v2

v3 whole, which is shorter than its diff:
```python
import jax
import jax.numpy as jnp
from jax import lax
from jax.experimental import pallas as pl
from jax.experimental.pallas import tpu as pltpu
from jax.sharding import PartitionSpec as P

LINES = 4096
OUTAGES = 8192
SCEN = 64
BUS_COLS = 2176
ROWS = 512
OUTS = 256
CHUNKS = ((0, 256), (256, 384), (640, 512), (1152, 512), (1664, 512))
F32 = jnp.float32
BF16 = jnp.bfloat16
NT = (((1,), (1,)), ((), ()))


def torus(size, step):
    return min(step, size - step)


PLANE = sorted(
    [(dy, dx) for dy in range(4) for dx in range(4) if dy + dx],
    key=lambda step: -torus(4, step[0]) - torus(4, step[1]),
)
COLUMN = sorted(
    [(dz, dc) for dz in range(8) for dc in range(2) if dz + dc], key=lambda step: -torus(8, step[0])
)


def split(value):
    high = value.astype(BF16)
    return high, (value - high.astype(F32)).astype(BF16)


def kernel(
    tier_hbm, inj_hbm, tf_hbm, w_hbm, ol_hbm, table_hbm, grad_ref, pen_ref,
    tier_ref, ol_ref, table_ref,
    tf, tf_hi, tf_lo, inj, inj_hl, w, w_t, w_parts, w_wide, limit_t, lane_hit, spread_in,
    part, s1, s2_src, s2, ol_src, ol_all, s3_src, s3, flow_src, flow_in, lane_of, tile_of,
    flow_t, outage_t, direct_t, back_rows, back_t,
    t1_src, t1, direct_src, direct_in, t2_src, t2, t3_src, t3, pen_src, pen1, pen2_src, pen2,
    g_src, r1, r2_src, r2,
    load_sem, send_sem, recv_sem, near_recv, far_back, core_send, core_recv, far_send, far_recv,
):
    i = lax.axis_index("line")
    j = lax.axis_index("bus")
    p = j // 2
    zh = lax.rem(j, 2)
    q = zh * 8 + i
    core = lax.rem(i, 2)
    z = i // 2
    half = lax.rem(p, 2)

    def plane_peer(step):
        other = lax.rem(p // 4 + step[0], 4) * 4 + lax.rem(p + step[1], 4)
        return other, (i, other * 2 + zh)

    def column_peer(step):
        chip = lax.rem(zh * 4 + z + step[0], 8)
        line = lax.rem(chip, 4) * 2 + lax.rem(core + step[1], 2)
        return (chip // 4) * 8 + line, (line, p * 2 + chip // 4)

    barrier = pltpu.get_barrier_semaphore()

    for peer, steps in ((plane_peer, PLANE), (column_peer, COLUMN)):
        for step in steps:
            pl.semaphore_signal(
                barrier, inc=1, device_id=peer(step)[1], device_id_type=pl.DeviceIdType.MESH
            )
    pairs = [(inj_hbm, inj)]
    pairs += [(tf_hbm.at[pl.ds(n * 128, 128)], tf.at[pl.ds(n * 128, 128)]) for n in range(4)]
    pairs += [(ol_hbm, ol_ref), (w_hbm, w), (table_hbm, table_ref), (tier_hbm, tier_ref)]
    loads = [pltpu.make_async_copy(a, b, load_sem.at[n]) for n, (a, b) in enumerate(pairs)]
    for copy in loads:
        copy.start()

    def send_all(peer, phase, source, target, arrived=None):
        for step in PLANE if peer is plane_peer else COLUMN:
            other, device = peer(step)
            pltpu.make_async_remote_copy(
                src_ref=source(other),
                dst_ref=target,
                send_sem=send_sem.at[phase],
                recv_sem=recv_sem.at[phase] if arrived is None else arrived,
                device_id=device,
                device_id_type=pl.DeviceIdType.MESH,
            ).start()

    def arrive_one(semaphore, view):
        pltpu.make_async_copy(view, view, semaphore).wait()

    def arrive(phase, buffer):
        view = buffer.at[pl.ds(0, 15)]
        pltpu.make_async_copy(view, view, recv_sem.at[phase]).wait()

    def sent(phase, buffer):
        view = buffer.at[pl.ds(0, 15)]
        pltpu.make_async_copy(view, view, send_sem.at[phase]).wait()


    loads[0].wait()
    inj_hi, inj_lo = split(inj[...])
    inj_hl[0:SCEN, :] = inj_hi
    inj_hl[SCEN : 2 * SCEN, :] = inj_lo
    for n in range(2):

        def cut(step, carry):
            rows = pl.ds(pl.multiple_of(step * 32, 32), 32)
            high, low = split(tf[rows, :])
            tf_hi[rows, :] = high
            tf_lo[rows, :] = low
            return carry

        for m in (2 * n, 2 * n + 1):
            loads[1 + m].wait()
            lax.fori_loop(4 * m, 4 * m + 4, cut, 0)
        rows = slice(n * 256, (n + 1) * 256)
        both = lax.dot_general(inj_hl[...], tf_hi[rows, :], NT, preferred_element_type=F32)
        low = lax.dot_general(inj_hl[0:SCEN, :], tf_lo[rows, :], NT, preferred_element_type=F32)
        flows = both[0:SCEN] + (both[SCEN : 2 * SCEN] + low)
        for group in range(8):
            part[2 * group + n] = flows[group * 8 : (group + 1) * 8]

    key_row = lax.broadcasted_iota(jnp.int32, (256, 256), 0)
    key_col = lax.broadcasted_iota(jnp.int32, (256, 256), 1)
    same_half = jnp.bitwise_and(jnp.right_shift(key_row, 5) - jnp.right_shift(key_col, 6), 1) == 0
    key = jnp.where(same_half, jnp.bitwise_and(key_row, 31) - jnp.right_shift(key_col, 7), -1)

    def widen_start():
        w_t[...] = w[...].T

        def group(g, carry):
            piece = w_t[pl.ds(pl.multiple_of(g * 32, 32), 32), :]
            high = piece.astype(BF16).astype(F32)
            rest = piece - high
            middle = rest.astype(BF16).astype(F32)
            stack = [
                value[:, h * 256 : (h + 1) * 256]
                for value in (high, middle, rest - middle)
                for h in range(2)
            ]
            stack.append(jnp.zeros((64, 256), F32))
            w_parts[g] = jnp.concatenate(stack, axis=0).T.astype(BF16)
            return carry

        lax.fori_loop(0, 8, group, 0)

    def widen(step, carry):
        ones = jnp.where(key == 2 * step, 1.0, 0.0).astype(BF16)
        for g in range(8):
            wide = jnp.dot(w_parts[g], ones, preferred_element_type=F32)
            w_wide[g * 32 + 2 * step] = wide[:, 0:128]
            w_wide[g * 32 + 2 * step + 1] = wide[:, 128:256]
        return carry

    pl.semaphore_wait(barrier, 30)
    send_all(plane_peer, 0, lambda other: part.at[other], s1.at[p])
    loads[5].wait()
    ol_src[...] = ol_ref[...].astype(F32)
    send_all(plane_peer, 1, lambda other: ol_src, ol_all.at[p])
    s1[p] = part[p]
    ol_all[p] = ol_src[...]
    for copy in loads[6:]:
        copy.wait()
    tiers = jnp.concatenate([tier_ref[...], tier_ref[...]], axis=1)
    left = lax.broadcasted_iota(jnp.int32, (128, 128), 1) < SCEN
    for block in range(2):
        rows = slice(block * 128, (block + 1) * 128)
        value = jnp.zeros((128, 128), F32)
        for tier in range(4):
            pair = [
                jnp.broadcast_to(
                    0.4 * table_ref[tier : tier + 1, h * 256 + block * 128 : h * 256 + block * 128 + 128].astype(F32),
                    (128, 128),
                ).T
                for h in range(2)
            ]
            value = jnp.where(tiers == tier, jnp.where(left, pair[0], pair[1]), value)
        limit_t[rows, :] = value
    widen_start()
    lax.fori_loop(0, 2, widen, 0)
    arrive(0, s1)
    s2_src[...] = jnp.sum(s1[...], axis=0)
    send_all(column_peer, 2, lambda other: s2_src, s2.at[q], near_recv.at[q])
    s2[q] = s2_src[...]
    arrive(1, ol_all)

    lax.fori_loop(2, 7, widen, 0)
    def names(group, carry):
        where = jnp.broadcast_to(ol_all[group], (8, 256)).astype(jnp.int32)
        lane_of[group] = jnp.bitwise_and(where, 127)
        tile_of[group] = jnp.right_shift(where, 7)
        return carry

    lax.fori_loop(0, 16, names, 0)
    for ahead in (2, 1, 3, 0):
        blocks = [lax.rem(z + ahead, 4) * 2 + c for c in range(2)]
        sources = []
        for block in blocks:
            for h in range(2):
                slot = h * 8 + block

                @pl.when(slot != q)
                def _():
                    arrive_one(near_recv.at[slot], s2.at[slot])

            full = s2[block] + s2[8 + block]
            for k in range(2):
                sources.append((block * 4 + 2 * half + k, full[:, k * 128 : (k + 1) * 128]))
        for group in range(16):
            for k in range(2):
                cols = slice(k * 128, (k + 1) * 128)
                lane = lane_of[group, :, cols]
                tile = tile_of[group, :, cols]
                out = jnp.zeros((8, 128), F32) if ahead == 2 else s3_src[group, :, cols]
                for name, source in sources:
                    out = jnp.where(tile == name, jnp.take_along_axis(source, lane, axis=1), out)
                s3_src[group, :, cols] = out
    flow_src[...] = s2[i] + s2[8 + i]
    send_all(plane_peer, 3, lambda other: s3_src.at[other], s3.at[p])
    send_all(plane_peer, 9, lambda other: flow_src, flow_in.at[p])
    s3[p] = s3_src[p]
    flow_in[p] = flow_src[...]
    lax.fori_loop(7, 16, widen, 0)
    arrive(3, s3)
    arrive(9, flow_in)
    tiles = jnp.concatenate([flow_in[2 * g + h] for h in range(2) for g in range(8)], axis=0)
    flow_t[...] = tiles.T
    picked = jnp.concatenate([s3[2 * g] + s3[2 * g + 1] for g in range(8)], axis=0)
    outage_t[...] = jnp.concatenate([picked, picked], axis=0).T

    penalty = jnp.zeros((8, 128), F32)
    for block in range(4):
        slabs = [slice(block * 64 + v * 8, block * 64 + v * 8 + 8) for v in range(8)]
        flow = [flow_t[rows, :] for rows in slabs]
        top = [limit_t[rows, :] for rows in slabs]
        low = [-value for value in top]

        def outages(step, carry):
            direct = list(carry[:8])
            squares = carry[8]
            eight = pl.ds(pl.multiple_of(step * 8, 8), 8)
            near = outage_t[eight, :]
            sums = []
            for u in range(8):
                name = step * 8 + u
                here = jnp.broadcast_to(near[u : u + 1, :], (8, 128))
                back = None
                for v in range(8):
                    factor = w_wide[name, slabs[v], :]
                    post = factor * here + flow[v]
                    over = post - jnp.minimum(jnp.maximum(post, low[v]), top[v])
                    direct[v] = direct[v] + over
                    term = over * factor
                    back = term if back is None else back + term
                    squares = squares + over * over
                if block > 0:
                    back = back + back_rows[name]
                if block < 3:
                    back_rows[name] = back
                else:
                    sums.append(jnp.sum(back, axis=0, keepdims=True))
            if block == 3:
                back_t[eight, :] = jnp.concatenate(sums, axis=0)
            return tuple(direct) + (squares,)

        start = tuple(jnp.zeros((8, 128), F32) for _ in range(8)) + (penalty,)
        result = lax.fori_loop(0, 32, outages, start)
        for v in range(8):
            direct_t[slabs[v], :] = result[v]
        penalty = result[8]

    back = back_t[...].T
    back = back[0:SCEN] + back[SCEN : 2 * SCEN]
    for g in range(8):
        t1_src[g] = back[g * 8 : (g + 1) * 8, :]
    send_all(plane_peer, 4, lambda other: t1_src.at[other // 2], t1.at[p], far_back.at[p])
    t1[p] = t1_src[p // 2]
    direct = direct_t[...].T
    for h in range(2):
        for g in range(8):
            direct_src[2 * g + h] = direct[h * SCEN + g * 8 : h * SCEN + g * 8 + 8, :]
    send_all(plane_peer, 10, lambda other: direct_src.at[other], direct_in.at[p])
    direct_in[p] = direct_src[p]
    pen_src[...] = jnp.sum(penalty, axis=0, keepdims=True)
    send_all(plane_peer, 5, lambda other: pen_src, pen1.at[p])
    pen1[p] = pen_src[...]
    def mark(group, carry):
        lane = jnp.bitwise_and(jnp.broadcast_to(ol_all[group], (128, 256)).astype(jnp.int32), 127)
        hit = lane == lax.broadcasted_iota(jnp.int32, (128, 256), 0)
        lane_hit[group] = jnp.where(hit, 1.0, 0.0).astype(BF16)
        return carry

    lax.fori_loop(0, 16, mark, 0)

    total = jnp.zeros((256, 128), F32)
    for step in [(0, 0)] + PLANE[::-1]:
        group = plane_peer(step)[0]
        if step != (0, 0):
            arrive_one(far_back.at[group], t1.at[group])
        high, low = split(t1[group])
        both = jnp.concatenate([high.astype(F32), low.astype(F32)], axis=0)
        tile = jnp.concatenate([tile_of[group], tile_of[group]], axis=0) - 2 * half
        for t in range(16):
            name = (t // 2) * 4 + t % 2
            spread_in[group, t * 16 : (t + 1) * 16, :] = jnp.where(tile == name, both, 0.0).astype(BF16)
        total = total + lax.dot_general(
            spread_in[group], lane_hit[group], NT, preferred_element_type=F32
        )
    for t in range(16):
        cols = slice((t % 2) * 128, (t % 2) * 128 + 128)
        t2_src[t // 2, :, cols] = total[t * 16 : t * 16 + 8] + total[t * 16 + 8 : t * 16 + 16]
    arrive(10, direct_in)
    t2_src[i] = t2_src[i] + jnp.sum(direct_in[...], axis=0)
    send_all(column_peer, 6, lambda other: t2_src.at[lax.rem(other, 8)], t2.at[q])
    t2[q] = t2_src[i]
    arrive(5, pen1)
    pen2_src[...] = jnp.sum(pen1[...], axis=0)
    send_all(column_peer, 7, lambda other: pen2_src, pen2.at[q])
    pen2[q] = pen2_src[...]
    arrive(6, t2)
    t3_src[...] = jnp.sum(t2[...], axis=0) * (2.0 / OUTAGES)
    send_all(plane_peer, 8, lambda other: t3_src, t3.at[p])
    t3[p] = t3_src[...]
    arrive(7, pen2)
    both = jnp.sum(pen2[...], axis=0) * (1.0 / (LINES * OUTAGES))
    pen_ref[...] = both[:, 0:SCEN] + both[:, SCEN:128]
    arrive(8, t3)

    grad = jnp.concatenate(
        [jnp.concatenate([t3[2 * g + h] for g in range(8)], axis=0) for h in range(2)], axis=1
    )
    grad_hi, grad_lo = split(grad)
    grad_hl = jnp.concatenate([grad_hi, grad_lo], axis=0)
    twin = (i + 1 - 2 * core, j)

    def core_copy(n):
        start, width = CHUNKS[n]
        cols = pl.ds(start, width)
        return pltpu.make_async_remote_copy(
            src_ref=g_src.at[1 - core, :, :, cols],
            dst_ref=r1.at[:, :, cols],
            send_sem=core_send.at[n],
            recv_sem=core_recv.at[n],
            device_id=twin,
            device_id_type=pl.DeviceIdType.MESH,
        )

    right = z // 2
    others = (3 - 3 * right, 2 - right, z + 1 - 2 * lax.rem(z, 2))

    def far_copy(n, d):
        start, width = CHUNKS[n]
        cols = pl.ds(start, width)
        return pltpu.make_async_remote_copy(
            src_ref=r2_src.at[others[d], :, cols],
            dst_ref=r2.at[z, :, cols],
            send_sem=far_send.at[n, d],
            recv_sem=far_recv.at[n, z],
            device_id=(others[d] * 2 + core, j),
            device_id_type=pl.DeviceIdType.MESH,
        )

    def pass_on(n):
        start, width = CHUNKS[n]
        cols = slice(start, start + width)
        core_copy(n).wait()
        r2_src[:, :, cols] = g_src[core, :, :, cols] + r1[:, :, cols]
        for d in range(3):
            far_copy(n, d).start()

    for n, (start, width) in enumerate(CHUNKS):
        cols = slice(start, start + width)
        both = jnp.dot(grad_hl, tf_hi[:, cols], preferred_element_type=F32)
        low = jnp.dot(grad_hi, tf_lo[:, cols], preferred_element_type=F32)
        out = both[0:SCEN] + (both[SCEN : 2 * SCEN] + low)
        for a in range(4):
            for c in range(2):
                row = (2 * a + c) * 8
                g_src[c, a, :, cols] = out[row : row + 8]
        core_copy(n).start()
        if n > 0:
            pass_on(n - 1)
    pass_on(len(CHUNKS) - 1)
    r2[z] = r2_src[z]
    for n in range(len(CHUNKS)):
        start, width = CHUNKS[n]
        for d in range(3):
            other = others[2 - d]
            arrive_one(far_recv.at[n, other], r2.at[other, :, pl.ds(start, width)])
            far_copy(n, d).wait_send()
    grad_ref[...] = (r2[0] + r2[1]) + (r2[2] + r2[3])
    for phase, buffer in enumerate((s1, ol_all, s2, s3, t1, pen1, t2, pen2, t3, flow_in, direct_in)):
        sent(phase, buffer)


def hand_over(grad_in, pen_in, grad_ref, pen_ref):
    grad_ref[...] = grad_in[...]
    pen_ref[...] = pen_in[...]


def body(injections, transfer_factors, outage_factors, outage_line, limit_table, scenario_tier):
    tile = (8, 256)
    vmem = pltpu.VMEM
    scratch = [
        vmem((1, SCEN), jnp.int32),
        vmem((1, OUTS), jnp.int32),
        vmem((4, ROWS), jnp.int32),
        vmem((ROWS, BUS_COLS), F32),
        vmem((ROWS, BUS_COLS), BF16),
        vmem((ROWS, BUS_COLS), BF16),
        vmem((SCEN, BUS_COLS), F32),
        vmem((2 * SCEN, BUS_COLS), BF16),
        vmem((ROWS, OUTS), F32),
        vmem((OUTS, ROWS), F32),
        vmem((8, 256, 256), BF16),
        vmem((OUTS, 256, 128), F32),
        vmem((256, 128), F32),
        vmem((16, 128, 256), BF16),
        vmem((16, 256, 256), BF16),
        vmem((16,) + tile, F32),
        vmem((16,) + tile, F32),
        vmem(tile, F32),
        vmem((16,) + tile, F32),
        vmem((1, OUTS), F32),
        vmem((16, 1, OUTS), F32),
        vmem((16,) + tile, F32),
        vmem((16,) + tile, F32),
        vmem(tile, F32),
        vmem((16,) + tile, F32),
        vmem((16,) + tile, jnp.int32),
        vmem((16,) + tile, jnp.int32),
        vmem((256, 128), F32),
        vmem((OUTS, 128), F32),
        vmem((256, 128), F32),
        vmem((OUTS, 8, 128), F32),
        vmem((OUTS, 128), F32),
        vmem((8,) + tile, F32),
        vmem((16,) + tile, F32),
        vmem((16,) + tile, F32),
        vmem((16,) + tile, F32),
        vmem((8,) + tile, F32),
        vmem((16,) + tile, F32),
        vmem(tile, F32),
        vmem((16,) + tile, F32),
        vmem((1, 128), F32),
        vmem((16, 1, 128), F32),
        vmem((1, 128), F32),
        vmem((16, 1, 128), F32),
        vmem((2, 4, 8, BUS_COLS), F32),
        vmem((4, 8, BUS_COLS), F32),
        vmem((4, 8, BUS_COLS), F32),
        vmem((4, 8, BUS_COLS), F32),
        pltpu.SemaphoreType.DMA((9,)),
        pltpu.SemaphoreType.DMA((11,)),
        pltpu.SemaphoreType.DMA((11,)),
        pltpu.SemaphoreType.DMA((16,)),
        pltpu.SemaphoreType.DMA((16,)),
        pltpu.SemaphoreType.DMA((5,)),
        pltpu.SemaphoreType.DMA((5,)),
        pltpu.SemaphoreType.DMA((5, 3)),
        pltpu.SemaphoreType.DMA((5, 4)),
    ]
    hbm = pl.BlockSpec(memory_space=pl.ANY)
    whole = pl.BlockSpec(memory_space=pltpu.VMEM)
    grad, penalty = pl.pallas_call(
        kernel,
        out_shape=(
            jax.ShapeDtypeStruct((8, BUS_COLS), F32),
            jax.ShapeDtypeStruct((1, SCEN), F32),
        ),
        in_specs=[hbm] * 6,
        out_specs=(whole, whole),
        scratch_shapes=scratch,
        compiler_params=pltpu.CompilerParams(
            collective_id=0, has_side_effects=True, vmem_limit_bytes=60 << 20
        ),
        name="overload",
    )(
        scenario_tier.reshape(1, SCEN),
        injections,
        transfer_factors,
        outage_factors,
        outage_line.reshape(1, OUTS),
        limit_table,
    )
    grad, penalty = pl.pallas_call(
        hand_over,
        out_shape=(
            jax.ShapeDtypeStruct((8, BUS_COLS), F32),
            jax.ShapeDtypeStruct((1, SCEN), F32),
        ),
        in_specs=[whole, whole],
        out_specs=(whole, whole),
        name="hand_over",
    )(grad, penalty)
    return grad, penalty.reshape(SCEN)


def solution(mesh):
    return jax.shard_map(
        body,
        mesh=mesh,
        in_specs=(
            P(None, "bus"),
            P("line", "bus"),
            P("line", "bus"),
            P("bus"),
            P(None, "line"),
            P(),
        ),
        out_specs=(P("line", "bus"), P()),
        check_vma=False,
    )
```

time: 74.8 us -> 70.7 us (0.945)
  local copies, waits for them, and re-layouts: 2.63 us -> 0 us
  Pallas kernels: 71.3 us -> 70 us
    pallas_call x1, Pallas kernels: 71.3 us -> 68.4 us  [body(): pl.pallas_call(kernel, out_shape=(jax.ShapeDtypeStruct((8, BUS_COLS), F32...]
    unnamed x2 -> x0, local copies, waits for them, and re-layouts: 2.63 us -> none
    pallas_call x0 -> x1, Pallas kernels: none -> 1.52 us  [body(): pl.pallas_call(hand_over, out_shape=(jax.ShapeDtypeStruct((8, BUS_COLS),...]
where the time goes in v3:
time: 70.7 us; the launch traced here: 70.6 us
  Pallas kernels  70 us (99%)
    pallas_call x1, Pallas kernels, body(): pl.pallas_call(kernel, out_shape=(jax.ShapeDtypeStruct((8, BUS_COLS), F32...  68.4 us
    pallas_call x1, Pallas kernels, body(): pl.pallas_call(hand_over, out_shape=(jax.ShapeDtypeStruct((8, BUS_COLS),...  1.52 us

profile of v3, /device:TPU:1, one launch (start us, length us, event | category | flops | bytes accessed | tf_op | source)
XLA Modules:
  0.0 70.6 jit_solution(718318745230748939)
XLA Ops:
  0.6 68.4 %overload.1 = (f32[8,2176]{1,0:T(8,128)}, f32[1,64]{1,0:T(1,128)}) custom-call(s32[1,64]{1,0:T(1,128)} %bitcast.4, f32[64,2176]{1,0:T(8,128)} %inj_hbm.1, f32[512,2176]{1,0:T(8,128)} %tf_hbm.1, f32[512,256]{1,0:T(8,128)} %w_hbm.1, s32[1,256]{1,0:T(1,128)} %bitcast.3, s32[4,512]{1,0:T(4,128)} %table_hbm.1), custom_call_target="tpu_custom_call" | custom-call | tf_op jit(solution)/shard_map/overload/pallas_call | solution.py:469
  69.1 1.5 %hand_over.1 = (f32[8,2176]{1,0:T(8,128)}, f32[1,64]{1,0:T(1,128)}) custom-call(f32[8,2176]{1,0:T(8,128)} %get-tuple-element.6.grad_in, f32[1,64]{1,0:T(1,128)} %get-tuple-element.7.pen_in), custom_call_target="tpu_custom_call" | custom-call | tf_op jit(solution)/shard_map/hand_over/pallas_call | solution.py:490

commit v4 on v3

--- a/solution.py
+++ b/solution.py
@@ -11,7 +11,7 @@
 BUS_COLS = 2176
 ROWS = 512
 OUTS = 256
-CHUNKS = ((0, 256), (256, 384), (640, 512), (1152, 512), (1664, 512))
+CHUNKS = ((0, 640), (640, 768), (1408, 768))
 F32 = jnp.float32
 BF16 = jnp.bfloat16
 NT = (((1,), (1,)), ((), ()))
@@ -42,8 +42,8 @@
     part, s1, s2_src, s2, ol_src, ol_all, s3_src, s3, flow_src, flow_in, lane_of, tile_of,
     flow_t, outage_t, direct_t, back_rows, back_t,
     t1_src, t1, direct_src, direct_in, t2_src, t2, t3_src, t3, pen_src, pen1, pen2_src, pen2,
-    g_src, r1, r2_src, r2,
-    load_sem, send_sem, recv_sem, near_recv, far_back, core_send, core_recv, far_send, far_recv,
+    r2_src, r2,
+    load_sem, send_sem, recv_sem, near_recv, far_back, t3_recv, pair_sem, far_send, far_recv,
 ):
     i = lax.axis_index("line")
     j = lax.axis_index("bus")
@@ -58,6 +58,10 @@
         other = lax.rem(p // 4 + step[0], 4) * 4 + lax.rem(p + step[1], 4)
         return other, (i, other * 2 + zh)
 
+    def cross_peer(step):
+        other, (line, bus) = plane_peer(step)
+        return other, (i + 1 - 2 * core, bus)
+
     def column_peer(step):
         chip = lax.rem(zh * 4 + z + step[0], 8)
         line = lax.rem(chip, 4) * 2 + lax.rem(core + step[1], 2)
@@ -65,7 +69,7 @@
 
     barrier = pltpu.get_barrier_semaphore()
 
-    for peer, steps in ((plane_peer, PLANE), (column_peer, COLUMN)):
+    for peer, steps in ((plane_peer, PLANE), (column_peer, COLUMN), (cross_peer, PLANE)):
         for step in steps:
             pl.semaphore_signal(
                 barrier, inc=1, device_id=peer(step)[1], device_id_type=pl.DeviceIdType.MESH
@@ -106,20 +110,14 @@
     inj_hl[0:SCEN, :] = inj_hi
     inj_hl[SCEN : 2 * SCEN, :] = inj_lo
     for n in range(2):
-
-        def cut(step, carry):
-            rows = pl.ds(pl.multiple_of(step * 32, 32), 32)
-            high, low = split(tf[rows, :])
-            tf_hi[rows, :] = high
-            tf_lo[rows, :] = low
-            return carry
-
         for m in (2 * n, 2 * n + 1):
             loads[1 + m].wait()
-            lax.fori_loop(4 * m, 4 * m + 4, cut, 0)
-        rows = slice(n * 256, (n + 1) * 256)
-        both = lax.dot_general(inj_hl[...], tf_hi[rows, :], NT, preferred_element_type=F32)
-        low = lax.dot_general(inj_hl[0:SCEN, :], tf_lo[rows, :], NT, preferred_element_type=F32)
+        high, low = split(tf[n * 256 : (n + 1) * 256, :])
+        rows = pl.ds(pl.multiple_of(core * ROWS + n * 256, 256), 256)
+        tf_hi[rows, :] = high
+        tf_lo[rows, :] = low
+        both = lax.dot_general(inj_hl[...], high, NT, preferred_element_type=F32)
+        low = lax.dot_general(inj_hl[0:SCEN, :], low, NT, preferred_element_type=F32)
         flows = both[0:SCEN] + (both[SCEN : 2 * SCEN] + low)
         for group in range(8):
             part[2 * group + n] = flows[group * 8 : (group + 1) * 8]
@@ -156,7 +154,7 @@
             w_wide[g * 32 + 2 * step + 1] = wide[:, 128:256]
         return carry
 
-    pl.semaphore_wait(barrier, 30)
+    pl.semaphore_wait(barrier, 45)
     send_all(plane_peer, 0, lambda other: part.at[other], s1.at[p])
     loads[5].wait()
     ol_src[...] = ol_ref[...].astype(F32)
@@ -232,6 +230,16 @@
     picked = jnp.concatenate([s3[2 * g] + s3[2 * g + 1] for g in range(8)], axis=0)
     outage_t[...] = jnp.concatenate([picked, picked], axis=0).T
 
+    pair = pltpu.make_async_remote_copy(
+        src_ref=tf_hbm,
+        dst_ref=tf,
+        send_sem=pair_sem.at[0],
+        recv_sem=pair_sem.at[1],
+        device_id=(i + 1 - 2 * core, j),
+        device_id_type=pl.DeviceIdType.MESH,
+    )
+    pair.start()
+
     penalty = jnp.zeros((8, 128), F32)
     for block in range(4):
         slabs = [slice(block * 64 + v * 8, block * 64 + v * 8 + 8) for v in range(8)]
@@ -295,9 +303,20 @@
         return carry
 
     lax.fori_loop(0, 16, mark, 0)
+    pair.wait()
+
+    def cut(step, carry):
+        rows = pl.ds(pl.multiple_of(step * 64, 64), 64)
+        high, low = split(tf[rows, :])
+        rows = pl.ds(pl.multiple_of((1 - core) * ROWS + step * 64, 64), 64)
+        tf_hi[rows, :] = high
+        tf_lo[rows, :] = low
+        return carry
+
+    lax.fori_loop(0, 8, cut, 0)
 
     total = jnp.zeros((256, 128), F32)
-    for step in [(0, 0)] + PLANE[::-1]:
+    for turn, step in enumerate([(0, 0)] + PLANE[::-1]):
         group = plane_peer(step)[0]
         if step != (0, 0):
             arrive_one(far_back.at[group], t1.at[group])
@@ -306,9 +325,9 @@
         tile = jnp.concatenate([tile_of[group], tile_of[group]], axis=0) - 2 * half
         for t in range(16):
             name = (t // 2) * 4 + t % 2
-            spread_in[group, t * 16 : (t + 1) * 16, :] = jnp.where(tile == name, both, 0.0).astype(BF16)
+            spread_in[turn % 4, t * 16 : (t + 1) * 16, :] = jnp.where(tile == name, both, 0.0).astype(BF16)
         total = total + lax.dot_general(
-            spread_in[group], lane_hit[group], NT, preferred_element_type=F32
+            spread_in[turn % 4], lane_hit[group], NT, preferred_element_type=F32
         )
     for t in range(16):
         cols = slice((t % 2) * 128, (t % 2) * 128 + 128)
@@ -323,32 +342,50 @@
     pen2[q] = pen2_src[...]
     arrive(6, t2)
     t3_src[...] = jnp.sum(t2[...], axis=0) * (2.0 / OUTAGES)
-    send_all(plane_peer, 8, lambda other: t3_src, t3.at[p])
-    t3[p] = t3_src[...]
+    target = lax.rem(p // 2, 2)
+    slot = core * 8 + (p // 4) * 2 + half
+
+    def hand(step):
+        other = plane_peer(step)[0]
+        return pltpu.make_async_remote_copy(
+            src_ref=t3_src,
+            dst_ref=t3.at[slot],
+            send_sem=send_sem.at[8],
+            recv_sem=t3_recv.at[slot],
+            device_id=(z * 2 + target, other * 2 + zh),
+            device_id_type=pl.DeviceIdType.MESH,
+        )
+
+    for step in PLANE:
+        hand(step).start()
+
+    @pl.when(target != core)
+    def _():
+        hand((0, 0)).start()
+
+    @pl.when(target == core)
+    def _():
+        t3[slot] = t3_src[...]
+
     arrive(7, pen2)
     both = jnp.sum(pen2[...], axis=0) * (1.0 / (LINES * OUTAGES))
     pen_ref[...] = both[:, 0:SCEN] + both[:, SCEN:128]
-    arrive(8, t3)
+    for n in range(16):
+
+        @pl.when(jnp.logical_or(slot != n, target != core))
+        def _():
+            arrive_one(t3_recv.at[n], t3.at[n])
 
     grad = jnp.concatenate(
-        [jnp.concatenate([t3[2 * g + h] for g in range(8)], axis=0) for h in range(2)], axis=1
+        [
+            jnp.concatenate([t3[c * 8 + a * 2 + h] for a in range(4)], axis=0)
+            for c in range(2)
+            for h in range(2)
+        ],
+        axis=1,
     )
     grad_hi, grad_lo = split(grad)
     grad_hl = jnp.concatenate([grad_hi, grad_lo], axis=0)
-    twin = (i + 1 - 2 * core, j)
-
-    def core_copy(n):
-        start, width = CHUNKS[n]
-        cols = pl.ds(start, width)
-        return pltpu.make_async_remote_copy(
-            src_ref=g_src.at[1 - core, :, :, cols],
-            dst_ref=r1.at[:, :, cols],
-            send_sem=core_send.at[n],
-            recv_sem=core_recv.at[n],
-            device_id=twin,
-            device_id_type=pl.DeviceIdType.MESH,
-        )
-
     right = z // 2
     others = (3 - 3 * right, 2 - right, z + 1 - 2 * lax.rem(z, 2))
 
@@ -364,27 +401,17 @@
             device_id_type=pl.DeviceIdType.MESH,
         )
 
-    def pass_on(n):
-        start, width = CHUNKS[n]
-        cols = slice(start, start + width)
-        core_copy(n).wait()
-        r2_src[:, :, cols] = g_src[core, :, :, cols] + r1[:, :, cols]
-        for d in range(3):
-            far_copy(n, d).start()
-
     for n, (start, width) in enumerate(CHUNKS):
         cols = slice(start, start + width)
         both = jnp.dot(grad_hl, tf_hi[:, cols], preferred_element_type=F32)
         low = jnp.dot(grad_hi, tf_lo[:, cols], preferred_element_type=F32)
-        out = both[0:SCEN] + (both[SCEN : 2 * SCEN] + low)
+        out = both[0:32] + (both[32:64] + low)
         for a in range(4):
-            for c in range(2):
-                row = (2 * a + c) * 8
-                g_src[c, a, :, cols] = out[row : row + 8]
-        core_copy(n).start()
-        if n > 0:
-            pass_on(n - 1)
-    pass_on(len(CHUNKS) - 1)
+            r2_src[a, :, cols] = out[a * 8 : (a + 1) * 8]
+        for d in range(2):
+            far_copy(n, d).start()
+    for n in range(len(CHUNKS)):
+        far_copy(n, 2).start()
     r2[z] = r2_src[z]
     for n in range(len(CHUNKS)):
         start, width = CHUNKS[n]
@@ -396,6 +423,10 @@
     for phase, buffer in enumerate((s1, ol_all, s2, s3, t1, pen1, t2, pen2, t3, flow_in, direct_in)):
         sent(phase, buffer)
 
+    @pl.when(target != core)
+    def _():
+        arrive_one(send_sem.at[8], t3.at[0])
+
 
 def hand_over(grad_in, pen_in, grad_ref, pen_ref):
     grad_ref[...] = grad_in[...]
@@ -410,8 +441,8 @@
         vmem((1, OUTS), jnp.int32),
         vmem((4, ROWS), jnp.int32),
         vmem((ROWS, BUS_COLS), F32),
-        vmem((ROWS, BUS_COLS), BF16),
-        vmem((ROWS, BUS_COLS), BF16),
+        vmem((2 * ROWS, BUS_COLS), BF16),
+        vmem((2 * ROWS, BUS_COLS), BF16),
         vmem((SCEN, BUS_COLS), F32),
         vmem((2 * SCEN, BUS_COLS), BF16),
         vmem((ROWS, OUTS), F32),
@@ -420,7 +451,7 @@
         vmem((OUTS, 256, 128), F32),
         vmem((256, 128), F32),
         vmem((16, 128, 256), BF16),
-        vmem((16, 256, 256), BF16),
+        vmem((4, 256, 256), BF16),
         vmem((16,) + tile, F32),
         vmem((16,) + tile, F32),
         vmem(tile, F32),
@@ -450,8 +481,6 @@
         vmem((16, 1, 128), F32),
         vmem((1, 128), F32),
         vmem((16, 1, 128), F32),
-        vmem((2, 4, 8, BUS_COLS), F32),
-        vmem((4, 8, BUS_COLS), F32),
         vmem((4, 8, BUS_COLS), F32),
         vmem((4, 8, BUS_COLS), F32),
         pltpu.SemaphoreType.DMA((9,)),
@@ -459,10 +488,10 @@
         pltpu.SemaphoreType.DMA((11,)),
         pltpu.SemaphoreType.DMA((16,)),
         pltpu.SemaphoreType.DMA((16,)),
-        pltpu.SemaphoreType.DMA((5,)),
-        pltpu.SemaphoreType.DMA((5,)),
-        pltpu.SemaphoreType.DMA((5, 3)),
-        pltpu.SemaphoreType.DMA((5, 4)),
+        pltpu.SemaphoreType.DMA((16,)),
+        pltpu.SemaphoreType.DMA((2,)),
+        pltpu.SemaphoreType.DMA((3, 3)),
+        pltpu.SemaphoreType.DMA((3, 4)),
     ]
     hbm = pl.BlockSpec(memory_space=pl.ANY)
     whole = pl.BlockSpec(memory_space=pltpu.VMEM)

time: 70.7 us -> 68.5 us (0.969)
  Pallas kernels: 70 us -> 67.8 us
    pallas_call x1, Pallas kernels: 68.4 us -> 66.2 us  [body(): pl.pallas_call(kernel, out_shape=(jax.ShapeDtypeStruct((8, BUS_COLS), F32...]
where the time goes in v4:
time: 68.5 us; the launch traced here: 68.4 us
  Pallas kernels  67.8 us (99%)
    pallas_call x1, Pallas kernels, body(): pl.pallas_call(kernel, out_shape=(jax.ShapeDtypeStruct((8, BUS_COLS), F32...  66.2 us
    pallas_call x1, Pallas kernels, body(): pl.pallas_call(hand_over, out_shape=(jax.ShapeDtypeStruct((8, BUS_COLS),...  1.52 us

profile of v4, /device:TPU:1, one launch (start us, length us, event | category | flops | bytes accessed | tf_op | source)
XLA Modules:
  0.0 68.4 jit_solution(4858509545191159411)
XLA Ops:
  0.6 66.2 %overload.1 = (f32[8,2176]{1,0:T(8,128)}, f32[1,64]{1,0:T(1,128)}) custom-call(s32[1,64]{1,0:T(1,128)} %bitcast.4, f32[64,2176]{1,0:T(8,128)} %inj_hbm.1, f32[512,2176]{1,0:T(8,128)} %tf_hbm.1, f32[512,256]{1,0:T(8,128)} %w_hbm.1, s32[1,256]{1,0:T(1,128)} %bitcast.3, s32[4,512]{1,0:T(4,128)} %table_hbm.1), custom_call_target="tpu_custom_call" | custom-call | tf_op jit(solution)/shard_map/overload/pallas_call | solution.py:498
  66.9 1.5 %hand_over.1 = (f32[8,2176]{1,0:T(8,128)}, f32[1,64]{1,0:T(1,128)}) custom-call(f32[8,2176]{1,0:T(8,128)} %get-tuple-element.6.grad_in, f32[1,64]{1,0:T(1,128)} %get-tuple-element.7.pen_in), custom_call_target="tpu_custom_call" | custom-call | tf_op jit(solution)/shard_map/hand_over/pallas_call | solution.py:519

commit v5 on v4

--- a/solution.py
+++ b/solution.py
@@ -179,14 +179,14 @@
             value = jnp.where(tiers == tier, jnp.where(left, pair[0], pair[1]), value)
         limit_t[rows, :] = value
     widen_start()
-    lax.fori_loop(0, 2, widen, 0)
+    lax.fori_loop(0, 3, widen, 0)
     arrive(0, s1)
     s2_src[...] = jnp.sum(s1[...], axis=0)
     send_all(column_peer, 2, lambda other: s2_src, s2.at[q], near_recv.at[q])
     s2[q] = s2_src[...]
     arrive(1, ol_all)
 
-    lax.fori_loop(2, 7, widen, 0)
+    lax.fori_loop(3, 9, widen, 0)
     def names(group, carry):
         where = jnp.broadcast_to(ol_all[group], (8, 256)).astype(jnp.int32)
         lane_of[group] = jnp.bitwise_and(where, 127)
@@ -222,7 +222,7 @@
     send_all(plane_peer, 9, lambda other: flow_src, flow_in.at[p])
     s3[p] = s3_src[p]
     flow_in[p] = flow_src[...]
-    lax.fori_loop(7, 16, widen, 0)
+    lax.fori_loop(9, 16, widen, 0)
     arrive(3, s3)
     arrive(9, flow_in)
     tiles = jnp.concatenate([flow_in[2 * g + h] for h in range(2) for g in range(8)], axis=0)
@@ -240,7 +240,7 @@
     )
     pair.start()
 
-    penalty = jnp.zeros((8, 128), F32)
+    penalty = [jnp.zeros((8, 128), F32)] * 4
     for block in range(4):
         slabs = [slice(block * 64 + v * 8, block * 64 + v * 8 + 8) for v in range(8)]
         flow = [flow_t[rows, :] for rows in slabs]
@@ -249,7 +249,7 @@
 
         def outages(step, carry):
             direct = list(carry[:8])
-            squares = carry[8]
+            squares = list(carry[8:])
             eight = pl.ds(pl.multiple_of(step * 8, 8), 8)
             near = outage_t[eight, :]
             sums = []
@@ -264,7 +264,7 @@
                     direct[v] = direct[v] + over
                     term = over * factor
                     back = term if back is None else back + term
-                    squares = squares + over * over
+                    squares[v % 4] = squares[v % 4] + over * over
                 if block > 0:
                     back = back + back_rows[name]
                 if block < 3:
@@ -273,13 +273,13 @@
                     sums.append(jnp.sum(back, axis=0, keepdims=True))
             if block == 3:
                 back_t[eight, :] = jnp.concatenate(sums, axis=0)
-            return tuple(direct) + (squares,)
-
-        start = tuple(jnp.zeros((8, 128), F32) for _ in range(8)) + (penalty,)
+            return tuple(direct) + tuple(squares)
+
+        start = tuple(jnp.zeros((8, 128), F32) for _ in range(8)) + tuple(penalty)
         result = lax.fori_loop(0, 32, outages, start)
         for v in range(8):
             direct_t[slabs[v], :] = result[v]
-        penalty = result[8]
+        penalty = result[8:]
 
     back = back_t[...].T
     back = back[0:SCEN] + back[SCEN : 2 * SCEN]
@@ -293,7 +293,8 @@
             direct_src[2 * g + h] = direct[h * SCEN + g * 8 : h * SCEN + g * 8 + 8, :]
     send_all(plane_peer, 10, lambda other: direct_src.at[other], direct_in.at[p])
     direct_in[p] = direct_src[p]
-    pen_src[...] = jnp.sum(penalty, axis=0, keepdims=True)
+    squares = (penalty[0] + penalty[1]) + (penalty[2] + penalty[3])
+    pen_src[...] = jnp.sum(squares, axis=0, keepdims=True)
     send_all(plane_peer, 5, lambda other: pen_src, pen1.at[p])
     pen1[p] = pen_src[...]
     def mark(group, carry):
@@ -428,11 +429,6 @@
         arrive_one(send_sem.at[8], t3.at[0])
 
 
-def hand_over(grad_in, pen_in, grad_ref, pen_ref):
-    grad_ref[...] = grad_in[...]
-    pen_ref[...] = pen_in[...]
-
-
 def body(injections, transfer_factors, outage_factors, outage_line, limit_table, scenario_tier):
     tile = (8, 256)
     vmem = pltpu.VMEM
@@ -498,8 +494,8 @@
     grad, penalty = pl.pallas_call(
         kernel,
         out_shape=(
-            jax.ShapeDtypeStruct((8, BUS_COLS), F32),
-            jax.ShapeDtypeStruct((1, SCEN), F32),
+            pltpu.VMEM((8, BUS_COLS), F32),
+            pltpu.VMEM((1, SCEN), F32),
         ),
         in_specs=[hbm] * 6,
         out_specs=(whole, whole),
@@ -516,16 +512,6 @@
         outage_line.reshape(1, OUTS),
         limit_table,
     )
-    grad, penalty = pl.pallas_call(
-        hand_over,
-        out_shape=(
-            jax.ShapeDtypeStruct((8, BUS_COLS), F32),
-            jax.ShapeDtypeStruct((1, SCEN), F32),
-        ),
-        in_specs=[whole, whole],
-        out_specs=(whole, whole),
-        name="hand_over",
-    )(grad, penalty)
     return grad, penalty.reshape(SCEN)
 
 

time: 68.5 us -> 68 us (level)
  Pallas kernels: 67.8 us -> 66.1 us
  local copies, waits for them, and re-layouts: 0 us -> 1.14 us
    pallas_call x2 -> x1, Pallas kernels: 67.8 us -> 66.1 us  [body(): pl.pallas_call(kernel, out_shape=(pltpu.VMEM((8, BUS_COLS), F32), pltpu.V...]
    unnamed x0 -> x2, local copies, waits for them, and re-layouts: none -> 1.14 us
where the time goes in v5:
time: 68 us; the launch traced here: 67.9 us
  Pallas kernels  66.1 us (97%)
  local copies, waits for them, and re-layouts  1.14 us (2%)
    pallas_call x1, Pallas kernels, body(): pl.pallas_call(kernel, out_shape=(pltpu.VMEM((8, BUS_COLS), F32), pltpu.V...  66.1 us

profile of v5, /device:TPU:1, one launch (start us, length us, event | category | flops | bytes accessed | tf_op | source)
XLA Modules:
  0.0 67.9 jit_solution(10937225263486159509)
XLA Ops:
  0.6 66.1 %overload.1 = (f32[8,2176]{1,0:T(8,128)S(1)}, f32[1,64]{1,0:T(1,128)S(1)}) custom-call(s32[1,64]{1,0:T(1,128)} %bitcast.5, f32[64,2176]{1,0:T(8,128)} %inj_hbm.1, f32[512,2176]{1,0:T(8,128)} %tf_hbm.1, f32[512,256]{1,0:T(8,128)} %w_hbm.1, s32[1,256]{1,0:T(1,128)} %bitcast.4, s32[4,512]{1,0:T(4,128)} %table_hbm.1), custom_call_target="tpu_custom_call" | custom-call | tf_op jit(solution)/shard_map/overload/pallas_call | solution.py:494
  66.8 0.6 copy.10
  67.4 0.5 copy.11

commit v6 on v5

--- a/solution.py
+++ b/solution.py
@@ -81,8 +81,8 @@
     for copy in loads:
         copy.start()
 
-    def send_all(peer, phase, source, target, arrived=None):
-        for step in PLANE if peer is plane_peer else COLUMN:
+    def send_all(peer, phase, source, target, arrived=None, steps=None):
+        for step in steps or (PLANE if peer is plane_peer else COLUMN):
             other, device = peer(step)
             pltpu.make_async_remote_copy(
                 src_ref=source(other),
@@ -208,6 +208,9 @@
             full = s2[block] + s2[8 + block]
             for k in range(2):
                 sources.append((block * 4 + 2 * half + k, full[:, k * 128 : (k + 1) * 128]))
+        if ahead == 0:
+            flow_src[...] = s2[i] + s2[8 + i]
+            send_all(plane_peer, 9, lambda other: flow_src, flow_in.at[p])
         for group in range(16):
             for k in range(2):
                 cols = slice(k * 128, (k + 1) * 128)
@@ -217,9 +220,7 @@
                 for name, source in sources:
                     out = jnp.where(tile == name, jnp.take_along_axis(source, lane, axis=1), out)
                 s3_src[group, :, cols] = out
-    flow_src[...] = s2[i] + s2[8 + i]
     send_all(plane_peer, 3, lambda other: s3_src.at[other], s3.at[p])
-    send_all(plane_peer, 9, lambda other: flow_src, flow_in.at[p])
     s3[p] = s3_src[p]
     flow_in[p] = flow_src[...]
     lax.fori_loop(9, 16, widen, 0)
@@ -333,9 +334,11 @@
     for t in range(16):
         cols = slice((t % 2) * 128, (t % 2) * 128 + 128)
         t2_src[t // 2, :, cols] = total[t * 16 : t * 16 + 8] + total[t * 16 + 8 : t * 16 + 16]
+    column = lambda other: t2_src.at[lax.rem(other, 8)]
+    send_all(column_peer, 6, column, t2.at[q], steps=[step for step in COLUMN if step != (4, 0)])
     arrive(10, direct_in)
     t2_src[i] = t2_src[i] + jnp.sum(direct_in[...], axis=0)
-    send_all(column_peer, 6, lambda other: t2_src.at[lax.rem(other, 8)], t2.at[q])
+    send_all(column_peer, 6, column, t2.at[q], steps=[(4, 0)])
     t2[q] = t2_src[i]
     arrive(5, pen1)
     pen2_src[...] = jnp.sum(pen1[...], axis=0)

time: 68 us -> 68.5 us (level)
  no operation moved by 1% of the time
where the time goes in v6:
time: 68.5 us; the launch traced here: 68.4 us
  Pallas kernels  66.6 us (97%)
  local copies, waits for them, and re-layouts  1.14 us (2%)
    pallas_call x1, Pallas kernels, body(): pl.pallas_call(kernel, out_shape=(pltpu.VMEM((8, BUS_COLS), F32), pltpu.V...  66.6 us

profile of v6, /device:TPU:1, one launch (start us, length us, event | category | flops | bytes accessed | tf_op | source)
XLA Modules:
  0.0 68.4 jit_solution(9157014568271952826)
XLA Ops:
  0.6 66.6 %overload.1 = (f32[8,2176]{1,0:T(8,128)S(1)}, f32[1,64]{1,0:T(1,128)S(1)}) custom-call(s32[1,64]{1,0:T(1,128)} %bitcast.5, f32[64,2176]{1,0:T(8,128)} %inj_hbm.1, f32[512,2176]{1,0:T(8,128)} %tf_hbm.1, f32[512,256]{1,0:T(8,128)} %w_hbm.1, s32[1,256]{1,0:T(1,128)} %bitcast.4, s32[4,512]{1,0:T(4,128)} %table_hbm.1), custom_call_target="tpu_custom_call" | custom-call | tf_op jit(solution)/shard_map/overload/pallas_call | solution.py:497
  67.3 0.6 copy.10
  67.9 0.5 copy.11

commit v7 on v5

--- a/solution.py
+++ b/solution.py
@@ -222,6 +222,13 @@
     send_all(plane_peer, 9, lambda other: flow_src, flow_in.at[p])
     s3[p] = s3_src[p]
     flow_in[p] = flow_src[...]
+    def mark(group, carry):
+        lane = jnp.bitwise_and(jnp.broadcast_to(ol_all[group], (128, 256)).astype(jnp.int32), 127)
+        hit = lane == lax.broadcasted_iota(jnp.int32, (128, 256), 0)
+        lane_hit[group] = jnp.where(hit, 1.0, 0.0).astype(BF16)
+        return carry
+
+    lax.fori_loop(0, 16, mark, 0)
     lax.fori_loop(9, 16, widen, 0)
     arrive(3, s3)
     arrive(9, flow_in)
@@ -297,24 +304,6 @@
     pen_src[...] = jnp.sum(squares, axis=0, keepdims=True)
     send_all(plane_peer, 5, lambda other: pen_src, pen1.at[p])
     pen1[p] = pen_src[...]
-    def mark(group, carry):
-        lane = jnp.bitwise_and(jnp.broadcast_to(ol_all[group], (128, 256)).astype(jnp.int32), 127)
-        hit = lane == lax.broadcasted_iota(jnp.int32, (128, 256), 0)
-        lane_hit[group] = jnp.where(hit, 1.0, 0.0).astype(BF16)
-        return carry
-
-    lax.fori_loop(0, 16, mark, 0)
-    pair.wait()
-
-    def cut(step, carry):
-        rows = pl.ds(pl.multiple_of(step * 64, 64), 64)
-        high, low = split(tf[rows, :])
-        rows = pl.ds(pl.multiple_of((1 - core) * ROWS + step * 64, 64), 64)
-        tf_hi[rows, :] = high
-        tf_lo[rows, :] = low
-        return carry
-
-    lax.fori_loop(0, 8, cut, 0)
 
     total = jnp.zeros((256, 128), F32)
     for turn, step in enumerate([(0, 0)] + PLANE[::-1]):
@@ -341,6 +330,17 @@
     pen2_src[...] = jnp.sum(pen1[...], axis=0)
     send_all(column_peer, 7, lambda other: pen2_src, pen2.at[q])
     pen2[q] = pen2_src[...]
+    pair.wait()
+
+    def cut(step, carry):
+        rows = pl.ds(pl.multiple_of(step * 64, 64), 64)
+        high, low = split(tf[rows, :])
+        rows = pl.ds(pl.multiple_of((1 - core) * ROWS + step * 64, 64), 64)
+        tf_hi[rows, :] = high
+        tf_lo[rows, :] = low
+        return carry
+
+    lax.fori_loop(0, 8, cut, 0)
     arrive(6, t2)
     t3_src[...] = jnp.sum(t2[...], axis=0) * (2.0 / OUTAGES)
     target = lax.rem(p // 2, 2)

time: 68 us -> 68 us (level)
  no operation moved by 1% of the time
where the time goes in v7:
time: 68 us; the launch traced here: 67.9 us
  Pallas kernels  66.1 us (97%)
  local copies, waits for them, and re-layouts  1.14 us (2%)
    pallas_call x1, Pallas kernels, body(): pl.pallas_call(kernel, out_shape=(pltpu.VMEM((8, BUS_COLS), F32), pltpu.V...  66.1 us

profile of v7, /device:TPU:1, one launch (start us, length us, event | category | flops | bytes accessed | tf_op | source)
XLA Modules:
  0.0 67.9 jit_solution(15807511229947527736)
XLA Ops:
  0.6 66.1 %overload.1 = (f32[8,2176]{1,0:T(8,128)S(1)}, f32[1,64]{1,0:T(1,128)S(1)}) custom-call(s32[1,64]{1,0:T(1,128)} %bitcast.5, f32[64,2176]{1,0:T(8,128)} %inj_hbm.1, f32[512,2176]{1,0:T(8,128)} %tf_hbm.1, f32[512,256]{1,0:T(8,128)} %w_hbm.1, s32[1,256]{1,0:T(1,128)} %bitcast.4, s32[4,512]{1,0:T(4,128)} %table_hbm.1), custom_call_target="tpu_custom_call" | custom-call | tf_op jit(solution)/shard_map/overload/pallas_call | solution.py:494
  66.8 0.6 copy.10
  67.4 0.5 copy.11
